TPU v7x, 32 devices: a whole 2x2x4 slice. The times are simulated.
32 devices in a mesh: sky: 2 (over x), vel: 16 (over z, y, core).
Axes of the slice: x: 2, y: 2, z: 4, core: 2. Of those that a mesh axis runs over, the one named last changes fastest.
Arguments:
- psi: bfloat16 [2, 512, 1024], P(None, 'vel', 'sky'), may hold values from -6 to 6
- phi: bfloat16 [2, 512, 1024], P(None, 'vel', 'sky'), may hold values from 0.25 to 4
- shifts: int32 [512, 2, 2], P('vel'), may hold values from -16 to 16, as said below
- tile_mask: int32 [2, 2], replicated, may hold values 0 or 1
Outputs:
- best: float32 [512, 1024], P('vel', 'sky')
Inputs may be any that keep to these rules, and one draw needn't show every extreme that they name: `shifts`: pixel offsets of an epoch's image; entry 0 is a row offset, entry 1 a column offset.
All inputs are finite; a program needn't handle non-finite values.
Results may differ from a plain program's by a relative error of at most 0.0003.
Values may be sent and summed in bfloat16 or wider, within the bound.
No kernel may reach another device: no remote copies, remote signals or barrier semaphores. Data moves between devices by JAX's collectives and lax.ppermute only.
A program may use at most 64 MiB of HBM per device.

v0:
```python
import jax
import jax.numpy as jnp
from jax import lax
from jax.sharding import PartitionSpec as P

MAXS = 16


def padded_2(block, sides, width):
    for axis, dim in sides:
        count = lax.axis_size(axis)
        forward = [(i, i + 1) for i in range(count - 1)]
        backward = [(target, source) for source, target in forward]
        low = lax.ppermute(
            lax.slice_in_dim(block, block.shape[dim] - width, None, axis=dim), axis, forward
        )
        high = lax.ppermute(lax.slice_in_dim(block, 0, width, axis=dim), axis, backward)
        block = jnp.concatenate([low, block, high], axis=dim)
    return block


def stack_best(padded, offset_table, height, breadth, margin):
    total_vel = offset_table.shape[0]
    epochs = padded.shape[1]
    per_step = 1
    while total_vel // per_step > 16 or total_vel % per_step:
        per_step += 1
    grouped = offset_table.reshape(total_vel // per_step, per_step, epochs, 2)

    def advance(record, offsets):
        for member in range(per_step):
            psi_total = jnp.zeros((height, breadth), jnp.float32)
            phi_total = jnp.zeros((height, breadth), jnp.float32)
            for epoch in range(epochs):
                row_at = margin + offsets[member, epoch, 0]
                col_at = margin + offsets[member, epoch, 1]
                psi_total = psi_total + lax.dynamic_slice(
                    padded[0, epoch], (row_at, col_at), (height, breadth)
                ).astype(jnp.float32)
                phi_total = phi_total + lax.dynamic_slice(
                    padded[1, epoch], (row_at, col_at), (height, breadth)
                ).astype(jnp.float32)
            record = jnp.maximum(record, psi_total / jnp.sqrt(jnp.maximum(phi_total, 1.0)))
        return (record, None)

    start = jnp.full((height, breadth), -1e30, jnp.float32)
    record, unused = lax.scan(advance, start, grouped)
    return record


def body(psi, phi, shifts, tile_mask):
    margin = MAXS
    height = psi.shape[1]
    breadth = psi.shape[2]
    sky_index = lax.axis_index("sky")
    keep = lax.dynamic_slice_in_dim(tile_mask, sky_index, 1, 1).astype(jnp.bfloat16)[:, :, None]
    stacked = jnp.stack([psi * keep, phi * keep])
    whole = lax.all_gather(stacked, "vel", axis=2, tiled=True)
    rimmed = padded_2(whole, (("sky", 3),), margin)
    padded = jnp.pad(rimmed, ((0, 0), (0, 0), (margin, margin), (0, 0)))
    full_height = rimmed.shape[2]
    record = stack_best(padded, shifts, full_height, breadth, margin)
    joined = lax.pmax(record, "vel")
    result = lax.dynamic_slice_in_dim(joined, lax.axis_index("vel") * height, height, 0)
    return result


def solution(mesh):
    placed = (P(None, "vel", "sky"), P(None, "vel", "sky"), P("vel", None, None), P())
    return jax.shard_map(
        body, mesh=mesh, in_specs=placed, out_specs=P("vel", "sky"), check_vma=False
    )
```

profile of v0, /device:TPU:1, one launch (start us, length us, event | category | flops | bytes accessed | tf_op | source)
XLA Modules:
  0.0 436.0 jit_solution(14862448438077397219)
XLA Ops:
  9.1 44.4 %all-gather.2.cloned.1.call-done = bf16[2,2,512,512]{3,2,1,0:T(8,128)(2,1)} async-done(((bf16[2,2,32,512]{3,2,1,0:T(8,128)(2,1)}), bf16[2,2,512,512]{3,2,1,0:T(8,128)(2,1)}) %all-gather.2.cloned.1.call-update) | async-done | bytes 2097168 | tf_op jit(solution)/shard_map/all_gather | solution.py:58
  53.5 1.4 fusion.10
  54.9 3.1 collective-permute-start
  58.1 1.3 collective-permute-start.1
  59.5 9.6 %collective-permute-done = bf16[2,2,512,16]{3,2,1,0:T(8,128)(2,1)S(1)} collective-permute-done((bf16[2,2,512,16]{3,2,1,0:T(8,128)(2,1)S(1)}, bf16[2,2,512,16]{3,2,1,0:T(8,128)(2,1)S(1)}, u32[]{:S(2)}, u32[]{:S(2)}) %collective-permute-start) | collective-permute-done | bytes 65568 | tf_op jit(solution)/shard_map/ppermute | solution.py:14
  69.1 3.9 collective-permute-done.1
  73.0 3.1 fusion.6
  76.2 259.3 %while.14 = (s32[]{:T(128)}, f32[512,512]{1,0:T(8,128)}, bf16[2,2,544,544]{3,2,1,0:T(8,128)(2,1)S(1)}, s32[16,2,2,2]{3,2,1,0:T(2,128)S(1)}, s32[]{:T(128)}, /*in...) while((s32[]{:T(128)}, f32[512,512]{1,0:T(8,128)}, bf16[2,2,544,544]{3,2,1,0:T(8,128)(2,1)S(1)}, ...), condition=%wide.region_1.2_spmd.clone, body=%wide.region_0.1_spmd.clone.sunk | while | flops 4980771 | bytes 19415732 | solution.py:47
  87.9 3.5 bitcast_maximum_fusion.3
  91.4 1.0 copy-done.1
  104.1 3.5 bitcast_maximum_fusion.3
  107.6 1.0 copy-done.1
  120.2 3.5 bitcast_maximum_fusion.3
  123.8 1.0 copy-done.1
  136.4 3.5 bitcast_maximum_fusion.3
  140.0 1.0 copy-done.1
  152.6 3.5 bitcast_maximum_fusion.3
  156.2 1.0 copy-done.1
  168.8 3.5 bitcast_maximum_fusion.3
  185.0 3.6 bitcast_maximum_fusion.3
  201.3 3.5 bitcast_maximum_fusion.3
  217.5 3.5 bitcast_maximum_fusion.3
  233.7 3.5 bitcast_maximum_fusion.3
  249.9 3.5 bitcast_maximum_fusion.3
  266.1 3.5 bitcast_maximum_fusion.3
  282.3 3.5 bitcast_maximum_fusion.3
  285.9 1.0 copy-done.1
  298.5 3.5 bitcast_maximum_fusion.3
  314.7 3.5 bitcast_maximum_fusion.3
  330.9 3.5 bitcast_maximum_fusion.3
  335.5 92.2 %all-reduce.3.cloned.1.call-done = f32[512,512]{1,0:T(8,128)} async-done(((f32[512,512]{1,0:T(8,128)}), f32[512,512]{1,0:T(8,128)}) %all-reduce.3.cloned.1.call-update) | async-done | bytes 1048592 | tf_op jit(solution)/shard_map/pmax | solution.py:63
  427.7 1.5 constant_dynamic-slice_fusion.1
  (117 shorter events, 42.4 us)
Async XLA Ops:
  6.5 52.8 %copy-start.2 = (s32[32,2,2]{0,2,1:T(2,128)S(1)}, s32[32,2,2]{0,2,1:T(2,128)}, u32[]{:S(2)}) copy-start(s32[32,2,2]{0,2,1:T(2,128)} %param.8) | copy-start | bytes 1540
  6.5 47.0 %all-gather.2.cloned.1.call-start = ((), (), s32[]{:S(2)}) async-start(), calls=%async_computation | async-start | bytes 2228224 | tf_op jit(solution)/shard_map/all_gather | solution.py:58
  9.1 418.6 %all-reduce.3.cloned.1.call-start = ((), (), s32[]{:S(2)}) async-start(), calls=%async_computation.1 | async-start | bytes 2097152 | tf_op jit(solution)/shard_map/pmax | solution.py:63
  54.9 14.2 %collective-permute-start = (bf16[2,2,512,16]{3,2,1,0:T(8,128)(2,1)S(1)}, bf16[2,2,512,16]{3,2,1,0:T(8,128)(2,1)S(1)}, u32[]{:S(2)}, u32[]{:S(2)}) collective-permute-start(bf16[2,2,512,16]{3,2,1,0:T(8,128)(2,1)S(1)} %get-tuple-element.122), channel_id=1, source_target_pairs={{0,16},{1,17},{2,18},{3,19},{4,20},{5,21},{6,22},{7,23},{8,24},{9,... | collective-permute-start | bytes 196616 | tf_op jit(solution)/shard_map/ppermute | solution.py:14
  58.1 15.0 %collective-permute-start.1 = (bf16[2,2,512,16]{3,2,1,0:T(8,128)(2,1)S(1)}, bf16[2,2,512,16]{3,2,1,0:T(8,128)(2,1)}, u32[]{:S(2)}, u32[]{:S(2)}) collective-permute-start(bf16[2,2,512,16]{3,2,1,0:T(8,128)(2,1)S(1)} %get-tuple-element.123), channel_id=1, source_target_pairs={{16,0},{17,1},{18,2},{19,3},{20,4},{21,5},{22,6},{23,7},{24,8},{25... | collective-permute-start | bytes 196616 | tf_op jit(solution)/shard_map/ppermute | solution.py:17
  86.6 1.2 copy-start
  91.4 1.0 copy-start.1
  102.8 1.2 copy-start
  107.6 1.0 copy-start.1
  119.0 1.2 copy-start
  123.8 1.0 copy-start.1
  135.2 1.2 copy-start
  140.0 1.0 copy-start.1
  151.4 1.2 copy-start
  156.2 1.0 copy-start.1
  167.6 1.2 copy-start
  172.4 1.0 copy-start.1
  183.8 1.2 copy-start
  188.6 1.0 copy-start.1
  200.0 1.2 copy-start
  204.8 1.0 copy-start.1
  216.3 1.2 copy-start
  221.0 1.0 copy-start.1
  232.5 1.2 copy-start
  237.2 1.0 copy-start.1
  248.7 1.2 copy-start
  264.9 1.2 copy-start
  281.1 1.2 copy-start
  285.9 1.0 copy-start.1
  297.3 1.2 copy-start
  313.5 1.2 copy-start
  329.7 1.2 copy-start
  (5 other events, 5.0 us)
Sparse Core Ops, SparseCore 0:
  9.5 43.9 all-gather.1
  335.6 92.0 all-reduce.2
where the time goes:
time: 440 us; the launch traced here: 436 us
  loops' own time  157 us (36%)
  waiting for transfers between devices  150 us (34%)
  other arithmetic  62.1 us (14%)
  local copies, waits for them, and re-layouts  48.6 us (11%)
  between operations  13.5 us (3%)
  starting transfers between devices  4.46 us (1%)
    another operation x1, loops' own time, stack_best(): record, unused = lax.scan(advance, start, grouped)  157 us
    pmax x1, waiting for transfers between devices, body(): joined = lax.pmax(record, 'vel')  92.2 us
    max x16, other arithmetic, advance(): jnp.maximum(record, psi_total / jnp.sqrt(jnp.maximum(phi_total, 1.0)))  56.5 us
    all_gather x1, waiting for transfers between devices, body(): whole = lax.all_gather(stacked, 'vel', axis=2, tiled=True)  44.4 us
    while x64, local copies, waits for them, and re-layouts  31.2 us
    slice x16, local copies, waits for them, and re-layouts, advance(): col_at = margin + offsets[member, epoch, 1]  10.5 us
    ppermute x1, waiting for transfers between devices, padded_2(): lax.ppermute(lax.slice_in_dim(block, block.shape[dim] - width, None, axis...  9.6 us
  transfers between devices with their start and end apart: 4, of which 4 were waited for; matrix products, arithmetic and copies ran while one was open for 0% of the time, Pallas kernels for 0%

commit v1 on v0

v1 whole, which is shorter than its diff:
```python
import functools

import jax
import jax.numpy as jnp
from jax import lax
from jax.experimental import pallas as pl
from jax.experimental.pallas import tpu as pltpu
from jax.sharding import PartitionSpec as P

MAXS = 16
LANES = 128
SUBLANES = 8


def search_kernel(pieces, n_sky, height, breadth, epochs, *refs):
    tables, refs = refs[:pieces], refs[pieces:]
    mask_ref, own_ref, above_ref, below_ref, left_ref, right_ref, best_ref, window, copies = refs
    spots = 2 * MAXS + 1
    rows = height + 2 * MAXS
    tiles = breadth // LANES
    sky = lax.axis_index("sky")

    for epoch in range(epochs):
        for image in range(2):
            at = (epoch, image)
            window[at + (slice(0, MAXS),)] = above_ref[at].astype(jnp.float32)
            window[at + (slice(MAXS + height, rows),)] = below_ref[at].astype(jnp.float32)
            mid = slice(MAXS, MAXS + height)
            window[at + (mid, slice(0, LANES))] = left_ref[at].astype(jnp.float32)
            window[at + (mid, slice(LANES, LANES + breadth))] = own_ref[at].astype(jnp.float32)
            window[at + (mid, slice(LANES + breadth, 2 * LANES + breadth))] = right_ref[at].astype(jnp.float32)

    lane = lax.broadcasted_iota(jnp.int32, (SUBLANES, LANES), 1)
    row_tiles = rows // SUBLANES

    def shift_columns(step, unused):
        epoch = step // (2 * row_tiles)
        image = (step // row_tiles) % 2
        row = pl.multiple_of((step % row_tiles) * SUBLANES, SUBLANES)
        found = []
        for tile in range(tiles + 2):
            at = sky + (0 if 0 < tile <= tiles else (-1 if tile == 0 else 1))
            inside = jnp.logical_and(at >= 0, at < n_sky)
            keep = jnp.where(inside, mask_ref[epoch, jnp.clip(at, 0, n_sky - 1)], 0).astype(jnp.float32)
            part = window[epoch, image, pl.ds(row, SUBLANES), tile * LANES:(tile + 1) * LANES]
            found.append(part * keep)
        for spot in range(spots):
            offset = spot - MAXS
            if offset == 0:
                outs = found[1:-1]
            elif offset > 0:
                turned = [pltpu.roll(part, LANES - offset, 1) for part in found[1:]]
                outs = [jnp.where(lane < LANES - offset, turned[t], turned[t + 1]) for t in range(tiles)]
            else:
                turned = [pltpu.roll(part, -offset, 1) for part in found[:-1]]
                outs = [jnp.where(lane >= -offset, turned[t + 1], turned[t]) for t in range(tiles)]
            for tile in range(tiles):
                slab = ((epoch * spots + spot) * 2 + image) * tiles + tile
                copies[pl.ds(pl.multiple_of(slab * rows + row, SUBLANES), SUBLANES), :] = outs[tile]
        return unused

    lax.fori_loop(0, epochs * 2 * row_tiles, shift_columns, 0)

    per_velocity = epochs * 2

    def velocity(table, index, group, best):
        bases = []
        for epoch in range(epochs):
            down = table[group, index * per_velocity + 2 * epoch]
            across = table[group, index * per_velocity + 2 * epoch + 1]
            bases.append((across + (MAXS + epoch * spots)) * (2 * tiles * rows) + down + MAXS)
        out = []
        for tile in range(tiles):
            psi_sum = sum(copies[pl.ds(base + tile * rows, height), :] for base in bases)
            phi_sum = sum(copies[pl.ds(base + (tiles + tile) * rows, height), :] for base in bases)
            out.append(jnp.maximum(best[tile], psi_sum * lax.rsqrt(jnp.maximum(phi_sum, 1.0))))
        return tuple(out)

    best = tuple(jnp.full((height, LANES), -1e30, jnp.float32) for _ in range(tiles))
    unroll = 4
    for table in tables:
        groups, width = table.shape
        count = width // per_velocity // unroll

        def steps(step, best):
            group, first = step // count, (step % count) * unroll
            for member in range(unroll):
                best = velocity(table, first + member, group, best)
            return best

        best = lax.fori_loop(0, groups * count, steps, best)
    for tile in range(tiles):
        best_ref[:, tile * LANES:(tile + 1) * LANES] = best[tile]


def gathered(piece, axis):
    count = lax.axis_size(axis)
    held, stride = piece, 1
    parts = [piece]
    while stride < count:
        radix = 4 if (count // stride) % 4 == 0 else 2
        if stride > 1:
            held = jnp.concatenate(parts, axis=0)
        parts = [held]
        for turn in range(1, radix):
            pairs = []
            for i in range(count):
                digit = (i // stride) % radix
                pairs.append((i, i + (((digit + turn) % radix) - digit) * stride))
            parts.append(lax.ppermute(held, axis, pairs))
        stride *= radix
    return parts


def body(psi, phi, shifts, tile_mask):
    epochs, height, breadth = psi.shape
    n_sky, n_vel = lax.axis_size("sky"), lax.axis_size("vel")
    own = jnp.stack([psi, phi], axis=1)
    sky_up = [(i, i + 1) for i in range(n_sky - 1)]
    sky_down = [(i + 1, i) for i in range(n_sky - 1)]
    left = lax.ppermute(own[..., breadth - LANES:], "sky", sky_up)
    right = lax.ppermute(own[..., :LANES], "sky", sky_down)
    tables = gathered(shifts.reshape(1, -1), "vel")
    wide = jnp.concatenate([left, own, right], axis=-1)
    vel_up = [(i, i + 1) for i in range(n_vel - 1)]
    vel_down = [(i + 1, i) for i in range(n_vel - 1)]
    above = lax.ppermute(wide[:, :, height - MAXS:], "vel", vel_up)
    below = lax.ppermute(wide[:, :, :MAXS], "vel", vel_down)
    vmem = pl.BlockSpec(memory_space=pltpu.VMEM)
    smem = pl.BlockSpec(memory_space=pltpu.SMEM)
    rows = height + 2 * MAXS
    slabs = epochs * (2 * MAXS + 1) * 2 * (breadth // LANES)
    return pl.pallas_call(
        functools.partial(search_kernel, len(tables), n_sky, height, breadth, epochs),
        out_shape=jax.ShapeDtypeStruct((height, breadth), jnp.float32),
        in_specs=[smem] * (len(tables) + 1) + [vmem] * 5,
        out_specs=vmem,
        scratch_shapes=[
            pltpu.VMEM((epochs, 2, rows, breadth + 2 * LANES), jnp.float32),
            pltpu.VMEM((slabs * rows, LANES), jnp.float32),
        ],
        compiler_params=pltpu.CompilerParams(vmem_limit_bytes=40 * 2**20),
        name="search",
    )(*tables, tile_mask, own, above, below, left, right)


def solution(mesh):
    placed = (P(None, "vel", "sky"), P(None, "vel", "sky"), P("vel", None, None), P())
    return jax.shard_map(
        body, mesh=mesh, in_specs=placed, out_specs=P("vel", "sky"), check_vma=False
    )
```

time: 440 us -> 48.6 us (0.11)
  the two profiles are of different devices: /device:TPU:1 before, /device:TPU:7 now
where the time goes in v1:
time: 48.6 us; the launch traced here: 48.4 us
  Pallas kernels  22.4 us (46%)
  starting transfers between devices  19.2 us (40%)
  waiting for transfers between devices  4.86 us (10%)
  local copies, waits for them, and re-layouts  0.98 us (2%)
  other arithmetic  0.85 us (2%)
    pallas_call x1, Pallas kernels, body(): pl.pallas_call(functools.partial(search_kernel, len(tables), n_sky, heigh...  22.4 us
    ppermute x6, starting transfers between devices, gathered(): parts.append(lax.ppermute(held, axis, pairs))  6.81 us
    ppermute x1, starting transfers between devices, body(): above = lax.ppermute(wide[:, :, height - MAXS:], 'vel', vel_up)  5.17 us
    ppermute x1, waiting for transfers between devices, body(): below = lax.ppermute(wide[:, :, :MAXS], 'vel', vel_down)  4.84 us
    ppermute x1, starting transfers between devices, body(): right = lax.ppermute(own[..., :LANES], 'sky', sky_down)  3.99 us
    ppermute x1, starting transfers between devices, body(): below = lax.ppermute(wide[:, :, :MAXS], 'vel', vel_down)  1.92 us
    ppermute x1, starting transfers between devices, body(): left = lax.ppermute(own[..., breadth - LANES:], 'sky', sky_up)  1.29 us
  transfers between devices with their start and end apart: 10, of which 1 were waited for; matrix products, arithmetic and copies ran while one was open for 2% of the time, Pallas kernels for 0%

profile of v1, /device:TPU:7, one launch (start us, length us, event | category | flops | bytes accessed | tf_op | source)
XLA Modules:
  0.0 48.4 jit_solution(15647747571015366532)
XLA Ops:
  0.0 0.0 copy-start.1
  0.0 0.8 %copy.6 = s32[32,2,2]{2,1,0:T(2,128)S(1)} copy(s32[32,2,2]{0,2,1:T(2,128)} %param.6) | data formatting | bytes 1024 | tf_op args[2]
  0.8 0.1 reshape.3
  1.0 0.8 %collective-permute-start = (s32[1,128]{1,0:T(1,128)S(1)}, s32[1,128]{1,0:T(1,128)S(1)}, u32[]{:S(2)}, u32[]{:S(2)}) collective-permute-start(s32[1,128]{1,0:T(1,128)S(1)} %reshape.3), channel_id=1, source_target_pairs={{0,1},{1,2},{2,3},{3,0},{4,5},{5,6},{6,7},{7,4},{8,9},{9,10},{10,1... | collective-permute-start | bytes 1544 | tf_op jit(solution)/shard_map/ppermute | solution.py:110
  1.8 1.2 %collective-permute-start.1 = (s32[1,128]{1,0:T(1,128)S(1)}, s32[1,128]{1,0:T(1,128)S(1)}, u32[]{:S(2)}, u32[]{:S(2)}) collective-permute-start(s32[1,128]{1,0:T(1,128)S(1)} %reshape.3), channel_id=1, source_target_pairs={{0,2},{1,3},{2,0},{3,1},{4,6},{5,7},{6,4},{7,5},{8,10},{9,11},{10,... | collective-permute-start | bytes 1544 | tf_op jit(solution)/shard_map/ppermute | solution.py:110
  3.0 0.0 collective-permute-start.2
  3.0 0.0 copy-done.1
  3.0 0.0 copy-start.2
  3.0 0.8 %fusion = (bf16[2,2,32,128]{3,2,1,0:T(8,128)(2,1)S(1)}, bf16[2,2,32,128]{3,2,1,0:T(8,128)(2,1)S(1)}) fusion(bf16[2,1,32,512]{3,2,1,0:T(8,128)(2,1)} %bitcast.5, bf16[2,1,32,512]{3,2,1,0:T(8,128)(2,1)S(1)} %bitcast.2), kind=kLoop, calls=%fused_computation.6 | loop fusion | flops 32768 | bytes 196608 | tf_op jit(solution)/shard_map/stack | solution.py:118
  3.9 1.3 %collective-permute-start.6 = (bf16[2,2,32,128]{3,2,1,0:T(8,128)(2,1)S(1)}, bf16[2,2,32,128]{3,2,1,0:T(8,128)(2,1)S(1)}, u32[]{:S(2)}, u32[]{:S(2)}) collective-permute-start(bf16[2,2,32,128]{3,2,1,0:T(8,128)(2,1)S(1)} %get-tuple-element.7), channel_id=1, source_target_pairs={{0,16},{1,17},{2,18},{3,19},{4,20},{5,21},{6,22},{7,23},{8,24},{9,... | collective-permute-start | bytes 98312 | tf_op jit(solution)/shard_map/ppermute | solution.py:121
  5.2 4.0 %collective-permute-start.7 = (bf16[2,2,32,128]{3,2,1,0:T(8,128)(2,1)S(1)}, bf16[2,2,32,128]{3,2,1,0:T(8,128)(2,1)S(1)}, u32[]{:S(2)}, u32[]{:S(2)}) collective-permute-start(bf16[2,2,32,128]{3,2,1,0:T(8,128)(2,1)S(1)} %get-tuple-element.8), channel_id=1, source_target_pairs={{16,0},{17,1},{18,2},{19,3},{20,4},{21,5},{22,6},{23,7},{24,8},{25... | collective-permute-start | bytes 98312 | tf_op jit(solution)/shard_map/ppermute | solution.py:122
  9.1 0.0 collective-permute-done
  9.2 0.0 collective-permute-done.1
  9.2 0.0 collective-permute-done.2
  9.2 1.3 %collective-permute-start.3 = (s32[4,128]{1,0:T(4,128)S(1)}, s32[4,128]{1,0:T(4,128)S(1)}, u32[]{:S(2)}, u32[]{:S(2)}) collective-permute-start(s32[4,128]{1,0:T(4,128)S(1)} %pad_add_fusion.refs_0_), channel_id=1, source_target_pairs={{0,4},{1,5},{2,6},{3,7},{4,8},{5,9},{6,10},{7,11},{8,12},{9,13},{1... | collective-permute-start | bytes 6152 | tf_op jit(solution)/shard_map/ppermute | solution.py:110
  10.5 2.3 %collective-permute-start.4 = (s32[4,128]{1,0:T(4,128)S(1)}, s32[4,128]{1,0:T(4,128)S(1)}, u32[]{:S(2)}, u32[]{:S(2)}) collective-permute-start(s32[4,128]{1,0:T(4,128)S(1)} %pad_add_fusion.refs_0_), channel_id=1, source_target_pairs={{0,8},{1,9},{2,10},{3,11},{4,12},{5,13},{6,14},{7,15},{8,0},{9,1},... | collective-permute-start | bytes 6152 | tf_op jit(solution)/shard_map/ppermute | solution.py:110
  12.9 1.1 %collective-permute-start.5 = (s32[4,128]{1,0:T(4,128)S(1)}, s32[4,128]{1,0:T(4,128)S(1)}, u32[]{:S(2)}, u32[]{:S(2)}) collective-permute-start(s32[4,128]{1,0:T(4,128)S(1)} %pad_add_fusion.refs_0_), channel_id=1, source_target_pairs={{0,12},{1,13},{2,14},{3,15},{4,0},{5,1},{6,2},{7,3},{8,4},{9,5},{1... | collective-permute-start | bytes 6152 | tf_op jit(solution)/shard_map/ppermute | solution.py:110
  13.9 0.0 collective-permute-done.6.refs_8_
  13.9 0.0 collective-permute-done.7.refs_9_
  13.9 0.0 copy-done.2
  14.0 5.2 %collective-permute-start.8 = (bf16[2,2,16,768]{3,2,1,0:T(8,128)(2,1)S(1)}, bf16[2,2,16,768]{3,2,1,0:T(8,128)(2,1)S(1)}, u32[]{:S(2)}, u32[]{:S(2)}) collective-permute-start(bf16[2,2,16,768]{3,2,1,0:T(8,128)(2,1)S(1)} %get-tuple-element.6), channel_id=1, source_target_pairs={{0,1},{1,2},{2,3},{3,4},{4,5},{5,6},{6,7},{7,8},{8,9},{9,10},{10,1... | collective-permute-start | bytes 294920 | tf_op jit(solution)/shard_map/ppermute | solution.py:127
  19.2 0.0 copy-start
  19.2 1.9 %collective-permute-start.9 = (bf16[2,2,16,768]{3,2,1,0:T(8,128)(2,1)S(1)}, bf16[2,2,16,768]{3,2,1,0:T(8,128)(2,1)S(1)}, u32[]{:S(2)}, u32[]{:S(2)}) collective-permute-start(bf16[2,2,16,768]{3,2,1,0:T(8,128)(2,1)S(1)} %get-tuple-element.5), channel_id=1, source_target_pairs={{1,0},{2,1},{3,2},{4,3},{5,4},{6,5},{7,6},{8,7},{9,8},{10,9},{11,1... | collective-permute-start | bytes 294920 | tf_op jit(solution)/shard_map/ppermute | solution.py:128
  21.1 0.0 collective-permute-done.3.refs_1_
  21.1 0.0 collective-permute-done.4.refs_2_
  21.1 0.0 collective-permute-done.5.refs_3_
  21.2 0.0 collective-permute-done.8.refs_6_
  21.2 4.8 %collective-permute-done.9.refs_7_ = bf16[2,2,16,768]{3,2,1,0:T(8,128)(2,1)S(1)} collective-permute-done((bf16[2,2,16,768]{3,2,1,0:T(8,128)(2,1)S(1)}, bf16[2,2,16,768]{3,2,1,0:T(8,128)(2,1)S(1)}, u32[]{:S(2)}, u32[]{:S(2)}) %collective-permute-start.9) | collective-permute-done | bytes 98336 | tf_op jit(solution)/shard_map/ppermute | solution.py:128
  26.0 0.0 copy-done
  26.0 22.4 %search.1 = f32[32,512]{1,0:T(8,128)} custom-call(s32[4,128]{1,0:T(4,128)S(1)} %pad_add_fusion.refs_0_, s32[4,128]{1,0:T(4,128)S(1)} %collective-permute-done.3.refs_1_, s32[4,128]{1,0:T(4,128)S(1)} %collective-permute-done.4.refs_2_, s32[4,128]{1,0:T(4,128)S(1)} %collective-permute-done.5.refs_3_, s32[2,2]{1,0:T(2,128)S(1)} %copy-done, ...), custom_call_target="tpu_custom_call" | custom-call | tf_op jit(solution)/shard_map/search/pallas_call | solution.py:133
  (4 shorter events, 0.1 us)
Async XLA Ops:
  0.0 3.0 %copy-start.1 = (bf16[2,32,512]{2,1,0:T(8,128)(2,1)S(1)}, bf16[2,32,512]{2,1,0:T(8,128)(2,1)}, u32[]{:S(2)}) copy-start(bf16[2,32,512]{2,1,0:T(8,128)(2,1)} %param.5) | copy-start | bytes 196612
  1.0 8.2 %collective-permute-start = (s32[1,128]{1,0:T(1,128)S(1)}, s32[1,128]{1,0:T(1,128)S(1)}, u32[]{:S(2)}, u32[]{:S(2)}) collective-permute-start(s32[1,128]{1,0:T(1,128)S(1)} %reshape.3), channel_id=1, source_target_pairs={{0,1},{1,2},{2,3},{3,0},{4,5},{5,6},{6,7},{7,4},{8,9},{9,10},{10,1... | collective-permute-start | bytes 1544 | tf_op jit(solution)/shard_map/ppermute | solution.py:110
  1.8 7.4 %collective-permute-start.1 = (s32[1,128]{1,0:T(1,128)S(1)}, s32[1,128]{1,0:T(1,128)S(1)}, u32[]{:S(2)}, u32[]{:S(2)}) collective-permute-start(s32[1,128]{1,0:T(1,128)S(1)} %reshape.3), channel_id=1, source_target_pairs={{0,2},{1,3},{2,0},{3,1},{4,6},{5,7},{6,4},{7,5},{8,10},{9,11},{10,... | collective-permute-start | bytes 1544 | tf_op jit(solution)/shard_map/ppermute | solution.py:110
  3.0 6.1 %collective-permute-start.2 = (s32[1,128]{1,0:T(1,128)S(1)}, s32[1,128]{1,0:T(1,128)S(1)}, u32[]{:S(2)}, u32[]{:S(2)}) collective-permute-start(s32[1,128]{1,0:T(1,128)S(1)} %reshape.3), channel_id=1, source_target_pairs={{0,3},{1,0},{2,1},{3,2},{4,7},{5,4},{6,5},{7,6},{8,11},{9,8},{10,9... | collective-permute-start | bytes 1544 | tf_op jit(solution)/shard_map/ppermute | solution.py:110
  3.0 10.9 %copy-start.2 = (bf16[2,32,512]{2,1,0:T(8,128)(2,1)S(1)}, bf16[2,32,512]{2,1,0:T(8,128)(2,1)}, u32[]{:S(2)}) copy-start(bf16[2,32,512]{2,1,0:T(8,128)(2,1)} %param.4) | copy-start | bytes 196612
  3.9 10.1 %collective-permute-start.6 = (bf16[2,2,32,128]{3,2,1,0:T(8,128)(2,1)S(1)}, bf16[2,2,32,128]{3,2,1,0:T(8,128)(2,1)S(1)}, u32[]{:S(2)}, u32[]{:S(2)}) collective-permute-start(bf16[2,2,32,128]{3,2,1,0:T(8,128)(2,1)S(1)} %get-tuple-element.7), channel_id=1, source_target_pairs={{0,16},{1,17},{2,18},{3,19},{4,20},{5,21},{6,22},{7,23},{8,24},{9,... | collective-permute-start | bytes 98312 | tf_op jit(solution)/shard_map/ppermute | solution.py:121
  5.2 8.8 %collective-permute-start.7 = (bf16[2,2,32,128]{3,2,1,0:T(8,128)(2,1)S(1)}, bf16[2,2,32,128]{3,2,1,0:T(8,128)(2,1)S(1)}, u32[]{:S(2)}, u32[]{:S(2)}) collective-permute-start(bf16[2,2,32,128]{3,2,1,0:T(8,128)(2,1)S(1)} %get-tuple-element.8), channel_id=1, source_target_pairs={{16,0},{17,1},{18,2},{19,3},{20,4},{21,5},{22,6},{23,7},{24,8},{25... | collective-permute-start | bytes 98312 | tf_op jit(solution)/shard_map/ppermute | solution.py:122
  9.2 11.9 %collective-permute-start.3 = (s32[4,128]{1,0:T(4,128)S(1)}, s32[4,128]{1,0:T(4,128)S(1)}, u32[]{:S(2)}, u32[]{:S(2)}) collective-permute-start(s32[4,128]{1,0:T(4,128)S(1)} %pad_add_fusion.refs_0_), channel_id=1, source_target_pairs={{0,4},{1,5},{2,6},{3,7},{4,8},{5,9},{6,10},{7,11},{8,12},{9,13},{1... | collective-permute-start | bytes 6152 | tf_op jit(solution)/shard_map/ppermute | solution.py:110
  10.5 10.6 %collective-permute-start.4 = (s32[4,128]{1,0:T(4,128)S(1)}, s32[4,128]{1,0:T(4,128)S(1)}, u32[]{:S(2)}, u32[]{:S(2)}) collective-permute-start(s32[4,128]{1,0:T(4,128)S(1)} %pad_add_fusion.refs_0_), channel_id=1, source_target_pairs={{0,8},{1,9},{2,10},{3,11},{4,12},{5,13},{6,14},{7,15},{8,0},{9,1},... | collective-permute-start | bytes 6152 | tf_op jit(solution)/shard_map/ppermute | solution.py:110
  12.9 8.3 %collective-permute-start.5 = (s32[4,128]{1,0:T(4,128)S(1)}, s32[4,128]{1,0:T(4,128)S(1)}, u32[]{:S(2)}, u32[]{:S(2)}) collective-permute-start(s32[4,128]{1,0:T(4,128)S(1)} %pad_add_fusion.refs_0_), channel_id=1, source_target_pairs={{0,12},{1,13},{2,14},{3,15},{4,0},{5,1},{6,2},{7,3},{8,4},{9,5},{1... | collective-permute-start | bytes 6152 | tf_op jit(solution)/shard_map/ppermute | solution.py:110
  14.0 7.2 %collective-permute-start.8 = (bf16[2,2,16,768]{3,2,1,0:T(8,128)(2,1)S(1)}, bf16[2,2,16,768]{3,2,1,0:T(8,128)(2,1)S(1)}, u32[]{:S(2)}, u32[]{:S(2)}) collective-permute-start(bf16[2,2,16,768]{3,2,1,0:T(8,128)(2,1)S(1)} %get-tuple-element.6), channel_id=1, source_target_pairs={{0,1},{1,2},{2,3},{3,4},{4,5},{5,6},{6,7},{7,8},{8,9},{9,10},{10,1... | collective-permute-start | bytes 294920 | tf_op jit(solution)/shard_map/ppermute | solution.py:127
  19.2 6.8 %copy-start = (s32[2,2]{1,0:T(2,128)S(1)}, s32[2,2]{1,0:T(2,128)}, u32[]{:S(2)}) copy-start(s32[2,2]{1,0:T(2,128)} %refs_4_.1) | copy-start | bytes 52
  19.2 6.8 %collective-permute-start.9 = (bf16[2,2,16,768]{3,2,1,0:T(8,128)(2,1)S(1)}, bf16[2,2,16,768]{3,2,1,0:T(8,128)(2,1)S(1)}, u32[]{:S(2)}, u32[]{:S(2)}) collective-permute-start(bf16[2,2,16,768]{3,2,1,0:T(8,128)(2,1)S(1)} %get-tuple-element.5), channel_id=1, source_target_pairs={{1,0},{2,1},{3,2},{4,3},{5,4},{6,5},{7,6},{8,7},{9,8},{10,9},{11,1... | collective-permute-start | bytes 294920 | tf_op jit(solution)/shard_map/ppermute | solution.py:128

commit v2 on v1

v2 whole, which is shorter than its diff:
```python
import functools

import jax
import jax.numpy as jnp
from jax import lax
from jax.experimental import pallas as pl
from jax.experimental.pallas import tpu as pltpu
from jax.sharding import PartitionSpec as P

MAXS = 16
LANES = 128
SUBLANES = 8


def search_kernel(pieces, n_sky, height, breadth, epochs, *refs):
    tables, refs = refs[:pieces], refs[pieces:]
    mask_ref, own_ref, near_ref, far_ref, *side_refs, best_ref, pairs, copies = refs
    spots = 2 * MAXS + 1
    rows = height + 2 * MAXS
    tiles = breadth // LANES
    images = epochs * 2
    sky = lax.axis_index("sky")
    even = lax.rem(lax.axis_index("vel"), 2) == 0
    near_row = jnp.where(even, MAXS + height, 0)
    far_row = MAXS + height - near_row

    for epoch in range(epochs):
        keeps = []
        for step in (-1, 0, 1):
            at = sky + step
            inside = jnp.logical_and(at >= 0, at < n_sky)
            keep = mask_ref[epoch, jnp.clip(at, 0, n_sky - 1)]
            keeps.append(jnp.where(inside, keep, 0).astype(jnp.float32))
        for image in range(2):
            first = (epoch * 2 + image) * rows
            for tile in range(tiles + 2):
                keep = keeps[0 if tile == 0 else 2 if tile == tiles + 1 else 1]
                if 0 < tile <= tiles:
                    columns = slice((tile - 1) * LANES, tile * LANES)
                    middle = own_ref[epoch, image, :, columns]
                else:
                    side = 0 if tile == 0 else len(side_refs) - 1
                    columns = slice(breadth + side * LANES, breadth + (side + 1) * LANES)
                    middle = side_refs[side][epoch, image]
                parts = (
                    (near_row, MAXS, near_ref[epoch, image, :, columns]),
                    (MAXS, height, middle),
                    (far_row, MAXS, far_ref[epoch, image, :, columns]),
                )
                for row, count, part in parts:
                    part = (part.astype(jnp.float32) * keep).astype(jnp.bfloat16)
                    place = pl.ds(pl.multiple_of(first + row, MAXS), count)
                    if tile > 0:
                        pairs[tile - 1, place, LANES:] = part
                    if tile <= tiles:
                        pairs[tile, place, :LANES] = part

    ahead = lax.broadcasted_iota(jnp.int32, (2 * LANES, LANES), 0) - lax.broadcasted_iota(
        jnp.int32, (2 * LANES, LANES), 1
    )
    depth = images * rows

    def mover(distance):
        return jnp.where(ahead == distance, 1.0, 0.0).astype(jnp.bfloat16)

    def two_spots(source, spot, distance):
        units = jnp.concatenate([mover(distance), mover(distance + 1)], axis=1)
        moved = jnp.dot(
            pairs[source:source + tiles].reshape(tiles * depth, 2 * LANES), units, preferred_element_type=jnp.float32
        )
        for k in range(2):
            at = pl.multiple_of((spot + k) * (tiles * depth), SUBLANES)
            copies[pl.ds(at, tiles * depth), :] = moved[:, k * LANES:(k + 1) * LANES]

    def before(step, unused):
        two_spots(0, 2 * step, 2 * step + LANES - MAXS)
        return unused

    def after(step, unused):
        two_spots(1, 2 * step + 1 + MAXS, 2 * step + 1)
        return unused

    lax.fori_loop(0, MAXS // 2, before, 0, unroll=8)
    lax.fori_loop(0, MAXS // 2, after, 0, unroll=8)
    for tile in range(tiles):
        at = MAXS * tiles * depth + tile * depth
        copies[at:at + depth, :] = pairs[tile, :, LANES:].astype(jnp.float32)

    def velocity(table, first, best):
        bases = []
        for epoch in range(epochs):
            down, across = table[first + 2 * epoch], table[first + 2 * epoch + 1]
            bases.append((across + MAXS) * (tiles * depth) + down + (MAXS + epoch * 2 * rows))
        out = []
        for tile in range(tiles):
            psi_sum = sum(copies[pl.ds(base + tile * depth, height), :] for base in bases)
            phi_sum = sum(copies[pl.ds(base + (tile * depth + rows), height), :] for base in bases)
            out.append(jnp.maximum(best[tile], psi_sum * lax.rsqrt(jnp.maximum(phi_sum, 1.0))))
        return tuple(out)

    best = tuple(jnp.full((height, LANES), -1e30, jnp.float32) for _ in range(tiles))
    unroll, each = 4, epochs * 2
    for table in tables:

        def steps(step, best):
            for member in range(unroll):
                best = velocity(table, (step * unroll + member) * each, best)
            return best

        best = lax.fori_loop(0, table.shape[0] // (unroll * each), steps, best)
    for tile in range(tiles):
        best_ref[:, tile * LANES:(tile + 1) * LANES] = best[tile]


def gathered(piece, axis):
    count = lax.axis_size(axis)
    stride, parts = count, [piece]
    while stride > 1:
        radix = 4 if stride % 4 == 0 else 2
        stride //= radix
        held = jnp.concatenate(parts) if len(parts) > 1 else parts[0]
        parts = [held]
        for turn in range(1, radix):
            pairs = []
            for i in range(count):
                digit = (i // stride) % radix
                pairs.append((i, i + ((digit + turn) % radix - digit) * stride))
            parts.append(lax.ppermute(held, axis, pairs))
    return parts


def body(psi, phi, shifts, tile_mask):
    epochs, height, breadth = psi.shape
    n_sky, n_vel = lax.axis_size("sky"), lax.axis_size("vel")
    own = jnp.stack([psi, phi], axis=1)
    first, last = own[..., :LANES], own[..., breadth - LANES:]
    if n_sky == 2:
        edge = jnp.where(lax.axis_index("sky") == 0, last, first)
        sides = [lax.ppermute(edge, "sky", [(0, 1), (1, 0)])]
    else:
        sides = [
            lax.ppermute(last, "sky", [(i, i + 1) for i in range(n_sky - 1)]),
            lax.ppermute(first, "sky", [(i + 1, i) for i in range(n_sky - 1)]),
        ]
    tables = gathered(shifts.reshape(-1), "vel")
    wide = jnp.concatenate([own, *sides], axis=-1)
    even = lax.rem(lax.axis_index("vel"), 2) == 0
    top, bottom = wide[:, :, :MAXS], wide[:, :, height - MAXS:]
    near = lax.ppermute(jnp.where(even, bottom, top), "vel", [(i, i ^ 1) for i in range(n_vel)])
    others = [(i, ((i + 1) ^ 1) - 1) for i in range(1, n_vel - 1)]
    far = lax.ppermute(jnp.where(even, top, bottom), "vel", others)
    vmem = pl.BlockSpec(memory_space=pltpu.VMEM)
    smem = pl.BlockSpec(memory_space=pltpu.SMEM)
    rows = height + 2 * MAXS
    slabs = epochs * (2 * MAXS + 1) * 2 * (breadth // LANES)
    return pl.pallas_call(
        functools.partial(search_kernel, len(tables), n_sky, height, breadth, epochs),
        out_shape=jax.ShapeDtypeStruct((height, breadth), jnp.float32),
        in_specs=[smem] * (len(tables) + 1) + [vmem] * (3 + len(sides)),
        out_specs=vmem,
        scratch_shapes=[
            pltpu.VMEM((breadth // LANES + 1, epochs * 2 * rows, 2 * LANES), jnp.bfloat16),
            pltpu.VMEM((slabs * rows, LANES), jnp.float32),
        ],
        compiler_params=pltpu.CompilerParams(vmem_limit_bytes=40 * 2**20),
        name="search",
    )(*tables, tile_mask, own, near, far, *sides)


def solution(mesh):
    placed = (P(None, "vel", "sky"), P(None, "vel", "sky"), P("vel", None, None), P())
    return jax.shard_map(
        body, mesh=mesh, in_specs=placed, out_specs=P("vel", "sky"), check_vma=False
    )
```

time: 48.6 us -> 33.9 us (0.70)
  the two profiles are of different devices: /device:TPU:7 before, /device:TPU:1 now
where the time goes in v2:
time: 33.9 us; the launch traced here: 33.7 us
  Pallas kernels  14.2 us (42%)
  starting transfers between devices  14.1 us (42%)
  waiting for transfers between devices  3.47 us (10%)
  local copies, waits for them, and re-layouts  1.03 us (3%)
  other arithmetic  0.86 us (3%)
    pallas_call x1, Pallas kernels, body(): pl.pallas_call(functools.partial(search_kernel, len(tables), n_sky, heigh...  14.2 us
    ppermute x6, starting transfers between devices, gathered(): parts.append(lax.ppermute(held, axis, pairs))  9 us
    ppermute x1, waiting for transfers between devices, body(): far = lax.ppermute(jnp.where(even, top, bottom), 'vel', others)  3.45 us
    ppermute x1, starting transfers between devices, body(): far = lax.ppermute(jnp.where(even, top, bottom), 'vel', others)  2.36 us
    ppermute x1, starting transfers between devices, body(): lax.ppermute(jnp.where(even, bottom, top), 'vel', [(i, i ^ 1) for i in ra...  1.45 us
    ppermute x1, starting transfers between devices, body(): sides = [lax.ppermute(edge, 'sky', [(0, 1), (1, 0)])]  1.28 us
    unnamed x10, local copies, waits for them, and re-layouts  0.86 us
    select_n x1, other arithmetic, body(): edge = jnp.where(lax.axis_index('sky') == 0, last, first)  0.8 us
  transfers between devices with their start and end apart: 9, of which 1 were waited for; matrix products, arithmetic and copies ran while one was open for 3% of the time, Pallas kernels for 0%

profile of v2, /device:TPU:1, one launch (start us, length us, event | category | flops | bytes accessed | tf_op | source)
XLA Modules:
  0.0 33.7 jit_solution(14688517159256060902)
XLA Ops:
  0.0 0.0 copy-start.1
  0.0 0.8 %copy.6 = s32[32,2,2]{2,1,0:T(2,128)S(1)} copy(s32[32,2,2]{0,2,1:T(2,128)} %param.6) | data formatting | bytes 1024 | tf_op args[2]
  0.8 0.1 reshape.3
  1.0 2.2 %collective-permute-start = (s32[128]{0:T(128)S(1)}, s32[128]{0:T(128)S(1)}, u32[]{:S(2)}, u32[]{:S(2)}) collective-permute-start(s32[128]{0:T(128)S(1)} %reshape.3), channel_id=1, source_target_pairs={{0,4},{1,5},{2,6},{3,7},{4,8},{5,9},{6,10},{7,11},{8,12},{9,13},{1... | collective-permute-start | bytes 1544 | tf_op jit(solution)/shard_map/ppermute | solution.py:128
  3.1 2.3 %collective-permute-start.1 = (s32[128]{0:T(128)S(1)}, s32[128]{0:T(128)S(1)}, u32[]{:S(2)}, u32[]{:S(2)}) collective-permute-start(s32[128]{0:T(128)S(1)} %reshape.3), channel_id=1, source_target_pairs={{0,8},{1,9},{2,10},{3,11},{4,12},{5,13},{6,14},{7,15},{8,0},{9,1},... | collective-permute-start | bytes 1544 | tf_op jit(solution)/shard_map/ppermute | solution.py:128
  5.4 1.1 %collective-permute-start.2 = (s32[128]{0:T(128)S(1)}, s32[128]{0:T(128)S(1)}, u32[]{:S(2)}, u32[]{:S(2)}) collective-permute-start(s32[128]{0:T(128)S(1)} %reshape.3), channel_id=1, source_target_pairs={{0,12},{1,13},{2,14},{3,15},{4,0},{5,1},{6,2},{7,3},{8,4},{9,5},{1... | collective-permute-start | bytes 1544 | tf_op jit(solution)/shard_map/ppermute | solution.py:128
  6.5 0.0 copy-done.1
  6.5 0.0 copy-start.2
  6.5 0.8 %fusion.1 = bf16[2,2,32,128]{3,2,1,0:T(8,128)(2,1)S(1)} fusion(bf16[2,1,32,512]{3,2,1,0:T(8,128)(2,1)} %bitcast.5, bf16[2,1,32,512]{3,2,1,0:T(8,128)(2,1)S(1)} %bitcast.2, pred[]{:T(512)S(6)} %eq.7), kind=kLoop, calls=%fused_computation.9 | loop fusion | flops 49152 | bytes 163841 | tf_op jit(solution)/shard_map/jit(_where)/select_n | solution.py:138
  7.3 1.3 %collective-permute-start.6 = (bf16[2,2,32,128]{3,2,1,0:T(8,128)(2,1)S(1)}, bf16[2,2,32,128]{3,2,1,0:T(8,128)(2,1)S(1)}, u32[]{:S(2)}, u32[]{:S(2)}) collective-permute-start(bf16[2,2,32,128]{3,2,1,0:T(8,128)(2,1)S(1)} %fusion.1), channel_id=1, source_target_pairs={{0,16},{16,0},{1,17},{17,1},{2,18},{18,2},{3,19},{19,3},{4,20},{20... | collective-permute-start | bytes 98312 | tf_op jit(solution)/shard_map/ppermute | solution.py:139
  8.6 0.0 collective-permute-done
  8.6 0.0 collective-permute-done.1
  8.7 0.0 collective-permute-done.2
  8.7 3.0 %collective-permute-start.3 = (s32[512]{0:T(512)S(1)}, s32[512]{0:T(512)S(1)}, u32[]{:S(2)}, u32[]{:S(2)}) collective-permute-start(s32[512]{0:T(512)S(1)} %constant_dynamic-update-slice_fusion.refs_0_), channel_id=1, source_target_pairs={{0,1},{1,2},{2,3},{3,0},{4,5},{5,6},{6,7},{7,4},{8,9},{9,10},{10,1... | collective-permute-start | bytes 6152 | tf_op jit(solution)/shard_map/ppermute | solution.py:128
  11.7 0.2 collective-permute-start.4
  11.9 0.2 collective-permute-start.5
  12.1 0.0 collective-permute-done.6.refs_8_
  12.1 0.0 copy-done.2
  12.2 1.5 %collective-permute-start.7 = (bf16[2,2,16,640]{3,2,1,0:T(8,128)(2,1)S(1)}, bf16[2,2,16,640]{3,2,1,0:T(8,128)(2,1)S(1)}, u32[]{:S(2)}, u32[]{:S(2)}) collective-permute-start(bf16[2,2,16,640]{3,2,1,0:T(8,128)(2,1)S(1)} %get-tuple-element.6), channel_id=1, source_target_pairs={{0,1},{1,0},{2,3},{3,2},{4,5},{5,4},{6,7},{7,6},{8,9},{9,8},{10,11... | collective-permute-start | bytes 245768 | tf_op jit(solution)/shard_map/ppermute | solution.py:149
  13.6 0.0 copy-start
  13.6 2.4 %collective-permute-start.8 = (bf16[2,2,16,640]{3,2,1,0:T(8,128)(2,1)S(1)}, bf16[2,2,16,640]{3,2,1,0:T(8,128)(2,1)S(1)}, u32[]{:S(2)}, u32[]{:S(2)}) collective-permute-start(bf16[2,2,16,640]{3,2,1,0:T(8,128)(2,1)S(1)} %get-tuple-element.5), channel_id=1, source_target_pairs={{1,2},{2,1},{3,4},{4,3},{5,6},{6,5},{7,8},{8,7},{9,10},{10,9},{11,... | collective-permute-start | bytes 245768 | tf_op jit(solution)/shard_map/ppermute | solution.py:151
  16.0 0.0 collective-permute-done.3.refs_1_
  16.0 0.0 collective-permute-done.4.refs_2_
  16.0 0.0 collective-permute-done.5.refs_3_
  16.1 0.0 collective-permute-done.7.refs_6_
  16.1 3.4 %collective-permute-done.8.refs_7_ = bf16[2,2,16,640]{3,2,1,0:T(8,128)(2,1)S(1)} collective-permute-done((bf16[2,2,16,640]{3,2,1,0:T(8,128)(2,1)S(1)}, bf16[2,2,16,640]{3,2,1,0:T(8,128)(2,1)S(1)}, u32[]{:S(2)}, u32[]{:S(2)}) %collective-permute-start.8) | collective-permute-done | bytes 81952 | tf_op jit(solution)/shard_map/ppermute | solution.py:151
  19.5 0.0 copy-done
  19.5 14.2 %search.1 = f32[32,512]{1,0:T(8,128)} custom-call(s32[512]{0:T(512)S(1)} %constant_dynamic-update-slice_fusion.refs_0_, s32[512]{0:T(512)S(1)} %collective-permute-done.3.refs_1_, s32[512]{0:T(512)S(1)} %collective-permute-done.4.refs_2_, s32[512]{0:T(512)S(1)} %collective-permute-done.5.refs_3_, s32[2,2]{1,0:T(2,128)S(1)} %copy-done, ...), custom_call_target="tpu_custom_call" | custom-call | tf_op jit(solution)/shard_map/search/pallas_call | solution.py:156
  (8 shorter events, 0.1 us)
Async XLA Ops:
  0.0 6.5 %copy-start.1 = (bf16[2,32,512]{2,1,0:T(8,128)(2,1)S(1)}, bf16[2,32,512]{2,1,0:T(8,128)(2,1)}, u32[]{:S(2)}) copy-start(bf16[2,32,512]{2,1,0:T(8,128)(2,1)} %param.5) | copy-start | bytes 196612
  1.0 7.7 %collective-permute-start = (s32[128]{0:T(128)S(1)}, s32[128]{0:T(128)S(1)}, u32[]{:S(2)}, u32[]{:S(2)}) collective-permute-start(s32[128]{0:T(128)S(1)} %reshape.3), channel_id=1, source_target_pairs={{0,4},{1,5},{2,6},{3,7},{4,8},{5,9},{6,10},{7,11},{8,12},{9,13},{1... | collective-permute-start | bytes 1544 | tf_op jit(solution)/shard_map/ppermute | solution.py:128
  3.1 5.5 %collective-permute-start.1 = (s32[128]{0:T(128)S(1)}, s32[128]{0:T(128)S(1)}, u32[]{:S(2)}, u32[]{:S(2)}) collective-permute-start(s32[128]{0:T(128)S(1)} %reshape.3), channel_id=1, source_target_pairs={{0,8},{1,9},{2,10},{3,11},{4,12},{5,13},{6,14},{7,15},{8,0},{9,1},... | collective-permute-start | bytes 1544 | tf_op jit(solution)/shard_map/ppermute | solution.py:128
  5.4 3.2 %collective-permute-start.2 = (s32[128]{0:T(128)S(1)}, s32[128]{0:T(128)S(1)}, u32[]{:S(2)}, u32[]{:S(2)}) collective-permute-start(s32[128]{0:T(128)S(1)} %reshape.3), channel_id=1, source_target_pairs={{0,12},{1,13},{2,14},{3,15},{4,0},{5,1},{6,2},{7,3},{8,4},{9,5},{1... | collective-permute-start | bytes 1544 | tf_op jit(solution)/shard_map/ppermute | solution.py:128
  6.5 5.6 %copy-start.2 = (bf16[2,32,512]{2,1,0:T(8,128)(2,1)S(1)}, bf16[2,32,512]{2,1,0:T(8,128)(2,1)}, u32[]{:S(2)}) copy-start(bf16[2,32,512]{2,1,0:T(8,128)(2,1)} %param.4) | copy-start | bytes 196612
  7.3 4.8 %collective-permute-start.6 = (bf16[2,2,32,128]{3,2,1,0:T(8,128)(2,1)S(1)}, bf16[2,2,32,128]{3,2,1,0:T(8,128)(2,1)S(1)}, u32[]{:S(2)}, u32[]{:S(2)}) collective-permute-start(bf16[2,2,32,128]{3,2,1,0:T(8,128)(2,1)S(1)} %fusion.1), channel_id=1, source_target_pairs={{0,16},{16,0},{1,17},{17,1},{2,18},{18,2},{3,19},{19,3},{4,20},{20... | collective-permute-start | bytes 98312 | tf_op jit(solution)/shard_map/ppermute | solution.py:139
  8.7 7.3 %collective-permute-start.3 = (s32[512]{0:T(512)S(1)}, s32[512]{0:T(512)S(1)}, u32[]{:S(2)}, u32[]{:S(2)}) collective-permute-start(s32[512]{0:T(512)S(1)} %constant_dynamic-update-slice_fusion.refs_0_), channel_id=1, source_target_pairs={{0,1},{1,2},{2,3},{3,0},{4,5},{5,6},{6,7},{7,4},{8,9},{9,10},{10,1... | collective-permute-start | bytes 6152 | tf_op jit(solution)/shard_map/ppermute | solution.py:128
  11.7 4.4 %collective-permute-start.4 = (s32[512]{0:T(512)S(1)}, s32[512]{0:T(512)S(1)}, u32[]{:S(2)}, u32[]{:S(2)}) collective-permute-start(s32[512]{0:T(512)S(1)} %constant_dynamic-update-slice_fusion.refs_0_), channel_id=1, source_target_pairs={{0,2},{1,3},{2,0},{3,1},{4,6},{5,7},{6,4},{7,5},{8,10},{9,11},{10,... | collective-permute-start | bytes 6152 | tf_op jit(solution)/shard_map/ppermute | solution.py:128
  11.9 4.2 %collective-permute-start.5 = (s32[512]{0:T(512)S(1)}, s32[512]{0:T(512)S(1)}, u32[]{:S(2)}, u32[]{:S(2)}) collective-permute-start(s32[512]{0:T(512)S(1)} %constant_dynamic-update-slice_fusion.refs_0_), channel_id=1, source_target_pairs={{0,3},{1,0},{2,1},{3,2},{4,7},{5,4},{6,5},{7,6},{8,11},{9,8},{10,9... | collective-permute-start | bytes 6152 | tf_op jit(solution)/shard_map/ppermute | solution.py:128
  12.2 3.9 %collective-permute-start.7 = (bf16[2,2,16,640]{3,2,1,0:T(8,128)(2,1)S(1)}, bf16[2,2,16,640]{3,2,1,0:T(8,128)(2,1)S(1)}, u32[]{:S(2)}, u32[]{:S(2)}) collective-permute-start(bf16[2,2,16,640]{3,2,1,0:T(8,128)(2,1)S(1)} %get-tuple-element.6), channel_id=1, source_target_pairs={{0,1},{1,0},{2,3},{3,2},{4,5},{5,4},{6,7},{7,6},{8,9},{9,8},{10,11... | collective-permute-start | bytes 245768 | tf_op jit(solution)/shard_map/ppermute | solution.py:149
  13.6 5.9 %copy-start = (s32[2,2]{1,0:T(2,128)S(1)}, s32[2,2]{1,0:T(2,128)}, u32[]{:S(2)}) copy-start(s32[2,2]{1,0:T(2,128)} %refs_4_.1) | copy-start | bytes 52
  13.6 5.9 %collective-permute-start.8 = (bf16[2,2,16,640]{3,2,1,0:T(8,128)(2,1)S(1)}, bf16[2,2,16,640]{3,2,1,0:T(8,128)(2,1)S(1)}, u32[]{:S(2)}, u32[]{:S(2)}) collective-permute-start(bf16[2,2,16,640]{3,2,1,0:T(8,128)(2,1)S(1)} %get-tuple-element.5), channel_id=1, source_target_pairs={{1,2},{2,1},{3,4},{4,3},{5,6},{6,5},{7,8},{8,7},{9,10},{10,9},{11,... | collective-permute-start | bytes 245768 | tf_op jit(solution)/shard_map/ppermute | solution.py:151

commit v3 on v2

--- a/solution.py
+++ b/solution.py
@@ -1,4 +1,5 @@
 import functools
+import operator
 
 import jax
 import jax.numpy as jnp
@@ -86,30 +87,34 @@
         at = MAXS * tiles * depth + tile * depth
         copies[at:at + depth, :] = pairs[tile, :, LANES:].astype(jnp.float32)
 
-    def velocity(table, first, best):
+    def velocity(table, count, index, best):
         bases = []
         for epoch in range(epochs):
-            down, across = table[first + 2 * epoch], table[first + 2 * epoch + 1]
+            down, across = table[2 * epoch * count + index], table[(2 * epoch + 1) * count + index]
             bases.append((across + MAXS) * (tiles * depth) + down + (MAXS + epoch * 2 * rows))
         out = []
-        for tile in range(tiles):
-            psi_sum = sum(copies[pl.ds(base + tile * depth, height), :] for base in bases)
-            phi_sum = sum(copies[pl.ds(base + (tile * depth + rows), height), :] for base in bases)
-            out.append(jnp.maximum(best[tile], psi_sum * lax.rsqrt(jnp.maximum(phi_sum, 1.0))))
+        for part in range(len(best)):
+            at = part // row_tiles * depth + part % row_tiles * SUBLANES
+            psi_sum = functools.reduce(operator.add, [copies[pl.ds(base + at, SUBLANES), :] for base in bases])
+            phi_sum = functools.reduce(operator.add, [copies[pl.ds(base + (at + rows), SUBLANES), :] for base in bases])
+            out.append(jnp.maximum(best[part], psi_sum * lax.rsqrt(jnp.maximum(phi_sum, 1.0))))
         return tuple(out)
 
-    best = tuple(jnp.full((height, LANES), -1e30, jnp.float32) for _ in range(tiles))
-    unroll, each = 4, epochs * 2
+    row_tiles = height // SUBLANES
+    best = tuple(jnp.full((SUBLANES, LANES), -1e30, jnp.float32) for _ in range(tiles * row_tiles))
+    unroll = 4
     for table in tables:
+        count = table.shape[0] // (2 * epochs)
 
         def steps(step, best):
             for member in range(unroll):
-                best = velocity(table, (step * unroll + member) * each, best)
+                best = velocity(table, count, step * unroll + member, best)
             return best
 
-        best = lax.fori_loop(0, table.shape[0] // (unroll * each), steps, best)
-    for tile in range(tiles):
-        best_ref[:, tile * LANES:(tile + 1) * LANES] = best[tile]
+        best = lax.fori_loop(0, count // unroll, steps, best)
+    for part in range(len(best)):
+        tile, row = part // row_tiles, part % row_tiles * SUBLANES
+        best_ref[row:row + SUBLANES, tile * LANES:(tile + 1) * LANES] = best[part]
 
 
 def gathered(piece, axis):
@@ -118,15 +123,12 @@
     while stride > 1:
         radix = 4 if stride % 4 == 0 else 2
         stride //= radix
-        held = jnp.concatenate(parts) if len(parts) > 1 else parts[0]
+        held = jnp.concatenate(parts, axis=-1) if len(parts) > 1 else piece
         parts = [held]
-        for turn in range(1, radix):
-            pairs = []
-            for i in range(count):
-                digit = (i // stride) % radix
-                pairs.append((i, i + ((digit + turn) % radix - digit) * stride))
+        for turn in range(radix - 1, 0, -1):
+            pairs = [(i, i ^ (turn * stride)) for i in range(count)]
             parts.append(lax.ppermute(held, axis, pairs))
-    return parts
+    return [jnp.concatenate([part.reshape(2 * part.shape[0], -1) for part in parts], axis=-1).reshape(-1)]
 
 
 def body(psi, phi, shifts, tile_mask):
@@ -142,7 +144,7 @@
             lax.ppermute(last, "sky", [(i, i + 1) for i in range(n_sky - 1)]),
             lax.ppermute(first, "sky", [(i + 1, i) for i in range(n_sky - 1)]),
         ]
-    tables = gathered(shifts.reshape(-1), "vel")
+    tables = gathered(jnp.transpose(shifts, (1, 2, 0)), "vel")
     wide = jnp.concatenate([own, *sides], axis=-1)
     even = lax.rem(lax.axis_index("vel"), 2) == 0
     top, bottom = wide[:, :, :MAXS], wide[:, :, height - MAXS:]

time: 33.9 us -> 31.4 us (0.926)
  starting transfers between devices: 14.1 us -> 12.8 us
  local copies, waits for them, and re-layouts: 1.03 us -> 0.02 us
  Pallas kernels: 14.2 us -> 13.5 us
    ppermute x1, starting transfers between devices: 1.45 us -> 0.33 us  [body(): lax.ppermute(jnp.where(even, bottom, top), 'vel', [(i, i ^ 1) for i in ra...]
    ppermute x6, waiting for transfers between devices: 0.02 us -> 1.13 us  [gathered(): parts.append(lax.ppermute(held, axis, pairs))]
    ppermute x6, starting transfers between devices: 9 us -> 8.15 us  [gathered(): parts.append(lax.ppermute(held, axis, pairs))]
    unnamed x10 -> x9, local copies, waits for them, and re-layouts: 0.86 us -> 0.02 us
    ppermute x1, waiting for transfers between devices: 3.45 us -> 2.61 us  [body(): far = lax.ppermute(jnp.where(even, top, bottom), 'vel', others)]
    ppermute x1, starting transfers between devices: 2.36 us -> 3.05 us  [body(): far = lax.ppermute(jnp.where(even, top, bottom), 'vel', others)]
    pallas_call x1, Pallas kernels: 14.2 us -> 13.5 us  [body(): pl.pallas_call(functools.partial(search_kernel, len(tables), n_sky, heigh...]
  transfers between devices with their start and end apart: 9 -> 9, of which waited for: 1 -> 2; matrix products, arithmetic and copies ran while one was open for 3% -> 3% of each run, Pallas kernels for 0% -> 0%
where the time goes in v3:
time: 31.4 us; the launch traced here: 31.2 us
  Pallas kernels  13.5 us (43%)
  starting transfers between devices  12.8 us (41%)
  waiting for transfers between devices  3.75 us (12%)
  other arithmetic  0.94 us (3%)
    pallas_call x1, Pallas kernels, body(): pl.pallas_call(functools.partial(search_kernel, len(tables), n_sky, heigh...  13.5 us
    ppermute x6, starting transfers between devices, gathered(): parts.append(lax.ppermute(held, axis, pairs))  8.15 us
    ppermute x1, starting transfers between devices, body(): far = lax.ppermute(jnp.where(even, top, bottom), 'vel', others)  3.05 us
    ppermute x1, waiting for transfers between devices, body(): far = lax.ppermute(jnp.where(even, top, bottom), 'vel', others)  2.61 us
    ppermute x1, starting transfers between devices, body(): sides = [lax.ppermute(edge, 'sky', [(0, 1), (1, 0)])]  1.27 us
    ppermute x6, waiting for transfers between devices, gathered(): parts.append(lax.ppermute(held, axis, pairs))  1.13 us
    select_n x1, other arithmetic, body(): edge = jnp.where(lax.axis_index('sky') == 0, last, first)  0.81 us
  transfers between devices with their start and end apart: 9, of which 2 were waited for; matrix products, arithmetic and copies ran while one was open for 3% of the time, Pallas kernels for 0%

profile of v3, /device:TPU:1, one launch (start us, length us, event | category | flops | bytes accessed | tf_op | source)
XLA Modules:
  0.0 31.2 jit_solution(12245975257877931500)
XLA Ops:
  0.0 4.2 %collective-permute-start = (s32[2,2,32]{2,1,0:T(2,128)}, s32[2,2,32]{2,1,0:T(2,128)S(1)}, u32[]{:S(2)}, u32[]{:S(2)}) collective-permute-start(s32[2,2,32]{2,1,0:T(2,128)} %bitcast.18), channel_id=1, source_target_pairs={{0,12},{1,13},{2,14},{3,15},{4,8},{5,9},{6,10},{7,11},{8,4},{9,5},... | collective-permute-start | bytes 1544 | tf_op jit(solution)/shard_map/ppermute | solution.py:130
  4.2 0.0 collective-permute-start.1
  4.2 0.3 collective-permute-start.2
  4.4 0.0 copy-start.1
  4.4 0.0 copy-start.2
  4.4 0.8 %fusion.1 = bf16[2,2,32,128]{3,2,1,0:T(8,128)(2,1)S(1)} fusion(bf16[2,1,32,512]{3,2,1,0:T(8,128)(2,1)} %bitcast.14, bf16[2,1,32,512]{3,2,1,0:T(8,128)(2,1)} %bitcast.11, pred[]{:T(512)S(6)} %eq.7), kind=kLoop, calls=%fused_computation.9 | loop fusion | flops 49152 | bytes 163841 | tf_op jit(solution)/shard_map/jit(_where)/select_n | solution.py:140
  5.3 1.3 %collective-permute-start.6 = (bf16[2,2,32,128]{3,2,1,0:T(8,128)(2,1)S(1)}, bf16[2,2,32,128]{3,2,1,0:T(8,128)(2,1)S(1)}, u32[]{:S(2)}, u32[]{:S(2)}) collective-permute-start(bf16[2,2,32,128]{3,2,1,0:T(8,128)(2,1)S(1)} %fusion.1), channel_id=1, source_target_pairs={{0,16},{16,0},{1,17},{17,1},{2,18},{18,2},{3,19},{19,3},{4,20},{20... | collective-permute-start | bytes 98312 | tf_op jit(solution)/shard_map/ppermute | solution.py:141
  6.5 0.0 copy-done.1
  6.5 0.0 copy-done.2
  6.6 0.0 copy-start.3
  6.6 0.0 collective-permute-done
  6.6 1.1 %collective-permute-done.1 = s32[2,2,32]{2,1,0:T(2,128)S(1)} collective-permute-done((s32[2,2,32]{2,1,0:T(2,128)}, s32[2,2,32]{2,1,0:T(2,128)S(1)}, u32[]{:S(2)}, u32[]{:S(2)}) %collective-permute-start.1) | collective-permute-done | bytes 544 | tf_op jit(solution)/shard_map/ppermute | solution.py:130
  7.7 0.0 collective-permute-done.2
  7.7 0.0 copy-done.3
  7.7 0.1 pad_add_fusion
  7.8 3.2 %collective-permute-start.3 = (s32[2,2,128]{2,1,0:T(2,128)S(1)}, s32[2,2,128]{2,1,0:T(2,128)S(1)}, u32[]{:S(2)}, u32[]{:S(2)}) collective-permute-start(s32[2,2,128]{2,1,0:T(2,128)S(1)} %pad_add_fusion), channel_id=1, source_target_pairs={{0,3},{1,2},{2,1},{3,0},{4,7},{5,6},{6,5},{7,4},{8,11},{9,10},{10,... | collective-permute-start | bytes 6152 | tf_op jit(solution)/shard_map/ppermute | solution.py:130
  11.0 0.2 collective-permute-start.4
  11.2 0.2 collective-permute-start.5
  11.5 0.0 collective-permute-done.6.refs_5_
  11.5 0.3 %collective-permute-start.7 = (bf16[2,2,16,640]{3,2,1,0:T(8,128)(2,1)S(1)}, bf16[2,2,16,640]{3,2,1,0:T(8,128)(2,1)S(1)}, u32[]{:S(2)}, u32[]{:S(2)}) collective-permute-start(bf16[2,2,16,640]{3,2,1,0:T(8,128)(2,1)S(1)} %get-tuple-element.6), channel_id=1, source_target_pairs={{0,1},{1,0},{2,3},{3,2},{4,5},{5,4},{6,7},{7,6},{8,9},{9,8},{10,11... | collective-permute-start | bytes 245768 | tf_op jit(solution)/shard_map/ppermute | solution.py:151
  11.9 3.0 %collective-permute-start.8 = (bf16[2,2,16,640]{3,2,1,0:T(8,128)(2,1)S(1)}, bf16[2,2,16,640]{3,2,1,0:T(8,128)(2,1)S(1)}, u32[]{:S(2)}, u32[]{:S(2)}) collective-permute-start(bf16[2,2,16,640]{3,2,1,0:T(8,128)(2,1)S(1)} %get-tuple-element.5), channel_id=1, source_target_pairs={{1,2},{2,1},{3,4},{4,3},{5,6},{6,5},{7,8},{8,7},{9,10},{10,9},{11,... | collective-permute-start | bytes 245768 | tf_op jit(solution)/shard_map/ppermute | solution.py:153
  14.9 0.0 collective-permute-done.3
  14.9 0.0 collective-permute-done.4
  14.9 0.0 collective-permute-done.5
  15.0 0.0 copy-start
  15.0 0.0 collective-permute-done.7.refs_3_
  15.0 2.6 %collective-permute-done.8.refs_4_ = bf16[2,2,16,640]{3,2,1,0:T(8,128)(2,1)S(1)} collective-permute-done((bf16[2,2,16,640]{3,2,1,0:T(8,128)(2,1)S(1)}, bf16[2,2,16,640]{3,2,1,0:T(8,128)(2,1)S(1)}, u32[]{:S(2)}, u32[]{:S(2)}) %collective-permute-start.8) | collective-permute-done | bytes 81952 | tf_op jit(solution)/shard_map/ppermute | solution.py:153
  17.6 0.0 copy-done
  17.6 13.5 %search.1 = f32[32,512]{1,0:T(8,128)} custom-call(s32[2048]{0:T(1024)S(1)} %bitcast.10, s32[2,2]{1,0:T(2,128)S(1)} %copy-done, bf16[2,2,32,512]{3,2,1,0:T(8,128)(2,1)S(1)} %pad_maximum_fusion.refs_2_, bf16[2,2,16,640]{3,2,1,0:T(8,128)(2,1)S(1)} %collective-permute-done.7.refs_3_, bf16[2,2,16,640]{3,2,1,0:T(8,128)(2,1)S(1)} %collective-permute-done.8.refs_4_, ...), custom_call_target="tpu_custom_call" | custom-call | tf_op jit(solution)/shard_map/search/pallas_call | solution.py:158
  (5 shorter events, 0.1 us)
Async XLA Ops:
  0.0 6.6 %collective-permute-start = (s32[2,2,32]{2,1,0:T(2,128)}, s32[2,2,32]{2,1,0:T(2,128)S(1)}, u32[]{:S(2)}, u32[]{:S(2)}) collective-permute-start(s32[2,2,32]{2,1,0:T(2,128)} %bitcast.18), channel_id=1, source_target_pairs={{0,12},{1,13},{2,14},{3,15},{4,8},{5,9},{6,10},{7,11},{8,4},{9,5},... | collective-permute-start | bytes 1544 | tf_op jit(solution)/shard_map/ppermute | solution.py:130
  4.2 3.5 %collective-permute-start.1 = (s32[2,2,32]{2,1,0:T(2,128)}, s32[2,2,32]{2,1,0:T(2,128)S(1)}, u32[]{:S(2)}, u32[]{:S(2)}) collective-permute-start(s32[2,2,32]{2,1,0:T(2,128)} %bitcast.19), channel_id=1, source_target_pairs={{0,8},{1,9},{2,10},{3,11},{4,12},{5,13},{6,14},{7,15},{8,0},{9,1},... | collective-permute-start | bytes 1544 | tf_op jit(solution)/shard_map/ppermute | solution.py:130
  4.2 3.5 %collective-permute-start.2 = (s32[2,2,32]{2,1,0:T(2,128)}, s32[2,2,32]{2,1,0:T(2,128)S(1)}, u32[]{:S(2)}, u32[]{:S(2)}) collective-permute-start(s32[2,2,32]{2,1,0:T(2,128)} %bitcast.20), channel_id=1, source_target_pairs={{0,4},{1,5},{2,6},{3,7},{4,0},{5,1},{6,2},{7,3},{8,12},{9,13},{10,... | collective-permute-start | bytes 1544 | tf_op jit(solution)/shard_map/ppermute | solution.py:130
  4.4 2.1 %copy-start.1 = (bf16[2,32,512]{2,1,0:T(8,128)(2,1)S(1)}, bf16[2,32,512]{2,1,0:T(8,128)(2,1)}, u32[]{:S(2)}) copy-start(bf16[2,32,512]{2,1,0:T(8,128)(2,1)} %param.5) | copy-start | bytes 196612
  4.4 2.1 %copy-start.2 = (bf16[2,32,512]{2,1,0:T(8,128)(2,1)S(1)}, bf16[2,32,512]{2,1,0:T(8,128)(2,1)}, u32[]{:S(2)}) copy-start(bf16[2,32,512]{2,1,0:T(8,128)(2,1)} %param.4) | copy-start | bytes 196612
  5.3 6.2 %collective-permute-start.6 = (bf16[2,2,32,128]{3,2,1,0:T(8,128)(2,1)S(1)}, bf16[2,2,32,128]{3,2,1,0:T(8,128)(2,1)S(1)}, u32[]{:S(2)}, u32[]{:S(2)}) collective-permute-start(bf16[2,2,32,128]{3,2,1,0:T(8,128)(2,1)S(1)} %fusion.1), channel_id=1, source_target_pairs={{0,16},{16,0},{1,17},{17,1},{2,18},{18,2},{3,19},{19,3},{4,20},{20... | collective-permute-start | bytes 98312 | tf_op jit(solution)/shard_map/ppermute | solution.py:141
  6.6 1.2 %copy-start.3 = (s32[32,2,2]{0,2,1:T(2,128)S(1)}, s32[32,2,2]{0,2,1:T(2,128)}, u32[]{:S(2)}) copy-start(s32[32,2,2]{0,2,1:T(2,128)} %param.6) | copy-start | bytes 1540
  7.8 7.1 %collective-permute-start.3 = (s32[2,2,128]{2,1,0:T(2,128)S(1)}, s32[2,2,128]{2,1,0:T(2,128)S(1)}, u32[]{:S(2)}, u32[]{:S(2)}) collective-permute-start(s32[2,2,128]{2,1,0:T(2,128)S(1)} %pad_add_fusion), channel_id=1, source_target_pairs={{0,3},{1,2},{2,1},{3,0},{4,7},{5,6},{6,5},{7,4},{8,11},{9,10},{10,... | collective-permute-start | bytes 6152 | tf_op jit(solution)/shard_map/ppermute | solution.py:130
  11.0 3.9 %collective-permute-start.4 = (s32[2,2,128]{2,1,0:T(2,128)S(1)}, s32[2,2,128]{2,1,0:T(2,128)S(1)}, u32[]{:S(2)}, u32[]{:S(2)}) collective-permute-start(s32[2,2,128]{2,1,0:T(2,128)S(1)} %pad_add_fusion), channel_id=1, source_target_pairs={{0,2},{1,3},{2,0},{3,1},{4,6},{5,7},{6,4},{7,5},{8,10},{9,11},{10,... | collective-permute-start | bytes 6152 | tf_op jit(solution)/shard_map/ppermute | solution.py:130
  11.2 3.7 %collective-permute-start.5 = (s32[2,2,128]{2,1,0:T(2,128)S(1)}, s32[2,2,128]{2,1,0:T(2,128)S(1)}, u32[]{:S(2)}, u32[]{:S(2)}) collective-permute-start(s32[2,2,128]{2,1,0:T(2,128)S(1)} %pad_add_fusion), channel_id=1, source_target_pairs={{0,1},{1,0},{2,3},{3,2},{4,5},{5,4},{6,7},{7,6},{8,9},{9,8},{10,11... | collective-permute-start | bytes 6152 | tf_op jit(solution)/shard_map/ppermute | solution.py:130
  11.5 3.5 %collective-permute-start.7 = (bf16[2,2,16,640]{3,2,1,0:T(8,128)(2,1)S(1)}, bf16[2,2,16,640]{3,2,1,0:T(8,128)(2,1)S(1)}, u32[]{:S(2)}, u32[]{:S(2)}) collective-permute-start(bf16[2,2,16,640]{3,2,1,0:T(8,128)(2,1)S(1)} %get-tuple-element.6), channel_id=1, source_target_pairs={{0,1},{1,0},{2,3},{3,2},{4,5},{5,4},{6,7},{7,6},{8,9},{9,8},{10,11... | collective-permute-start | bytes 245768 | tf_op jit(solution)/shard_map/ppermute | solution.py:151
  11.9 5.7 %collective-permute-start.8 = (bf16[2,2,16,640]{3,2,1,0:T(8,128)(2,1)S(1)}, bf16[2,2,16,640]{3,2,1,0:T(8,128)(2,1)S(1)}, u32[]{:S(2)}, u32[]{:S(2)}) collective-permute-start(bf16[2,2,16,640]{3,2,1,0:T(8,128)(2,1)S(1)} %get-tuple-element.5), channel_id=1, source_target_pairs={{1,2},{2,1},{3,4},{4,3},{5,6},{6,5},{7,8},{8,7},{9,10},{10,9},{11,... | collective-permute-start | bytes 245768 | tf_op jit(solution)/shard_map/ppermute | solution.py:153
  15.0 2.6 %copy-start = (s32[2,2]{1,0:T(2,128)S(1)}, s32[2,2]{1,0:T(2,128)}, u32[]{:S(2)}) copy-start(s32[2,2]{1,0:T(2,128)} %refs_1_.1) | copy-start | bytes 52

commit v4 on v3

--- a/solution.py
+++ b/solution.py
@@ -13,9 +13,8 @@
 SUBLANES = 8
 
 
-def search_kernel(pieces, n_sky, height, breadth, epochs, *refs):
-    tables, refs = refs[:pieces], refs[pieces:]
-    mask_ref, own_ref, near_ref, far_ref, *side_refs, best_ref, pairs, copies = refs
+def search_kernel(n_sky, height, breadth, epochs, *refs):
+    table, mask_ref, own_ref, near_ref, far_ref, *side_refs, best_ref, pairs, copies = refs
     spots = 2 * MAXS + 1
     rows = height + 2 * MAXS
     tiles = breadth // LANES
@@ -87,7 +86,7 @@
         at = MAXS * tiles * depth + tile * depth
         copies[at:at + depth, :] = pairs[tile, :, LANES:].astype(jnp.float32)
 
-    def velocity(table, count, index, best):
+    def velocity(count, index, best):
         bases = []
         for epoch in range(epochs):
             down, across = table[2 * epoch * count + index], table[(2 * epoch + 1) * count + index]
@@ -103,15 +102,14 @@
     row_tiles = height // SUBLANES
     best = tuple(jnp.full((SUBLANES, LANES), -1e30, jnp.float32) for _ in range(tiles * row_tiles))
     unroll = 4
-    for table in tables:
-        count = table.shape[0] // (2 * epochs)
+    count = table.shape[0] // (2 * epochs)
 
-        def steps(step, best):
-            for member in range(unroll):
-                best = velocity(table, count, step * unroll + member, best)
-            return best
+    def steps(step, best):
+        for member in range(unroll):
+            best = velocity(count, step * unroll + member, best)
+        return best
 
-        best = lax.fori_loop(0, count // unroll, steps, best)
+    best = lax.fori_loop(0, count // unroll, steps, best)
     for part in range(len(best)):
         tile, row = part // row_tiles, part % row_tiles * SUBLANES
         best_ref[row:row + SUBLANES, tile * LANES:(tile + 1) * LANES] = best[part]
@@ -119,16 +117,15 @@
 
 def gathered(piece, axis):
     count = lax.axis_size(axis)
-    stride, parts = count, [piece]
-    while stride > 1:
-        radix = 4 if stride % 4 == 0 else 2
-        stride //= radix
+    stride, parts = 1, [piece]
+    while stride < count:
+        radix = 4 if count // stride % 4 == 0 else 2
         held = jnp.concatenate(parts, axis=-1) if len(parts) > 1 else piece
         parts = [held]
         for turn in range(radix - 1, 0, -1):
-            pairs = [(i, i ^ (turn * stride)) for i in range(count)]
-            parts.append(lax.ppermute(held, axis, pairs))
-    return [jnp.concatenate([part.reshape(2 * part.shape[0], -1) for part in parts], axis=-1).reshape(-1)]
+            parts.append(lax.ppermute(held, axis, [(i, i ^ (turn * stride)) for i in range(count)]))
+        stride *= radix
+    return jnp.concatenate(parts, axis=-1).reshape(-1)
 
 
 def body(psi, phi, shifts, tile_mask):
@@ -144,7 +141,7 @@
             lax.ppermute(last, "sky", [(i, i + 1) for i in range(n_sky - 1)]),
             lax.ppermute(first, "sky", [(i + 1, i) for i in range(n_sky - 1)]),
         ]
-    tables = gathered(jnp.transpose(shifts, (1, 2, 0)), "vel")
+    table = gathered(jnp.transpose(shifts, (1, 2, 0)), "vel")
     wide = jnp.concatenate([own, *sides], axis=-1)
     even = lax.rem(lax.axis_index("vel"), 2) == 0
     top, bottom = wide[:, :, :MAXS], wide[:, :, height - MAXS:]
@@ -156,9 +153,9 @@
     rows = height + 2 * MAXS
     slabs = epochs * (2 * MAXS + 1) * 2 * (breadth // LANES)
     return pl.pallas_call(
-        functools.partial(search_kernel, len(tables), n_sky, height, breadth, epochs),
+        functools.partial(search_kernel, n_sky, height, breadth, epochs),
         out_shape=jax.ShapeDtypeStruct((height, breadth), jnp.float32),
-        in_specs=[smem] * (len(tables) + 1) + [vmem] * (3 + len(sides)),
+        in_specs=[smem] * 2 + [vmem] * (3 + len(sides)),
         out_specs=vmem,
         scratch_shapes=[
             pltpu.VMEM((breadth // LANES + 1, epochs * 2 * rows, 2 * LANES), jnp.bfloat16),
@@ -166,7 +163,7 @@
         ],
         compiler_params=pltpu.CompilerParams(vmem_limit_bytes=40 * 2**20),
         name="search",
-    )(*tables, tile_mask, own, near, far, *sides)
+    )(table, tile_mask, own, near, far, *sides)
 
 
 def solution(mesh):

time: 31.4 us -> 30.6 us (0.975)
  waiting for transfers between devices: 3.75 us -> 2.66 us
  local copies, waits for them, and re-layouts: 0.02 us -> 0.66 us
  starting transfers between devices: 12.8 us -> 12.4 us
    ppermute x6, starting transfers between devices: 8.15 us -> 6.75 us  [gathered(): lax.ppermute(held, axis, [(i, i ^ turn * stride) for i in range(count)])]
    ppermute x1, starting transfers between devices: 0.33 us -> 1.36 us  [body(): lax.ppermute(jnp.where(even, bottom, top), 'vel', [(i, i ^ 1) for i in ra...]
    ppermute x6, waiting for transfers between devices: 1.13 us -> 0.14 us  [gathered(): lax.ppermute(held, axis, [(i, i ^ turn * stride) for i in range(count)])]
    unnamed x9, local copies, waits for them, and re-layouts: 0.02 us -> 0.57 us
where the time goes in v4:
time: 30.6 us; the launch traced here: 30.3 us
  Pallas kernels  13.6 us (44%)
  starting transfers between devices  12.4 us (41%)
  waiting for transfers between devices  2.66 us (9%)
  other arithmetic  0.94 us (3%)
  local copies, waits for them, and re-layouts  0.66 us (2%)
    pallas_call x1, Pallas kernels, body(): pl.pallas_call(functools.partial(search_kernel, n_sky, height, breadth, e...  13.6 us
    ppermute x6, starting transfers between devices, gathered(): lax.ppermute(held, axis, [(i, i ^ turn * stride) for i in range(count)])  6.75 us
    ppermute x1, starting transfers between devices, body(): far = lax.ppermute(jnp.where(even, top, bottom), 'vel', others)  3.05 us
    ppermute x1, waiting for transfers between devices, body(): far = lax.ppermute(jnp.where(even, top, bottom), 'vel', others)  2.52 us
    ppermute x1, starting transfers between devices, body(): lax.ppermute(jnp.where(even, bottom, top), 'vel', [(i, i ^ 1) for i in ra...  1.36 us
    ppermute x1, starting transfers between devices, body(): sides = [lax.ppermute(edge, 'sky', [(0, 1), (1, 0)])]  1.27 us
    select_n x1, other arithmetic, body(): edge = jnp.where(lax.axis_index('sky') == 0, last, first)  0.81 us
  transfers between devices with their start and end apart: 9, of which 2 were waited for; matrix products, arithmetic and copies ran while one was open for 3% of the time, Pallas kernels for 0%

profile of v4, /device:TPU:1, one launch (start us, length us, event | category | flops | bytes accessed | tf_op | source)
XLA Modules:
  0.0 30.3 jit_solution(9994745947172723446)
XLA Ops:
  0.0 2.6 %collective-permute-start = (s32[2,2,32]{2,1,0:T(2,128)}, s32[2,2,32]{2,1,0:T(2,128)S(1)}, u32[]{:S(2)}, u32[]{:S(2)}) collective-permute-start(s32[2,2,32]{2,1,0:T(2,128)} %bitcast.13), channel_id=1, source_target_pairs={{0,3},{1,2},{2,1},{3,0},{4,7},{5,6},{6,5},{7,4},{8,11},{9,10},{10,... | collective-permute-start | bytes 1544 | tf_op jit(solution)/shard_map/ppermute | solution.py:126
  2.6 0.0 collective-permute-start.1
  2.6 0.4 %collective-permute-start.2 = (s32[2,2,32]{2,1,0:T(2,128)}, s32[2,2,32]{2,1,0:T(2,128)S(1)}, u32[]{:S(2)}, u32[]{:S(2)}) collective-permute-start(s32[2,2,32]{2,1,0:T(2,128)} %bitcast.15), channel_id=1, source_target_pairs={{0,1},{1,0},{2,3},{3,2},{4,5},{5,4},{6,7},{7,6},{8,9},{9,8},{10,11... | collective-permute-start | bytes 1544 | tf_op jit(solution)/shard_map/ppermute | solution.py:126
  3.1 0.0 copy-start.1
  3.1 0.0 copy-start.2
  3.1 0.8 %fusion.1 = bf16[2,2,32,128]{3,2,1,0:T(8,128)(2,1)S(1)} fusion(bf16[2,1,32,512]{3,2,1,0:T(8,128)(2,1)} %bitcast.9, bf16[2,1,32,512]{3,2,1,0:T(8,128)(2,1)} %bitcast.6, pred[]{:T(512)S(6)} %eq.7), kind=kLoop, calls=%fused_computation.9 | loop fusion | flops 49152 | bytes 163841 | tf_op jit(solution)/shard_map/jit(_where)/select_n | solution.py:137
  3.9 1.3 %collective-permute-start.6 = (bf16[2,2,32,128]{3,2,1,0:T(8,128)(2,1)S(1)}, bf16[2,2,32,128]{3,2,1,0:T(8,128)(2,1)S(1)}, u32[]{:S(2)}, u32[]{:S(2)}) collective-permute-start(bf16[2,2,32,128]{3,2,1,0:T(8,128)(2,1)S(1)} %fusion.1), channel_id=1, source_target_pairs={{0,16},{16,0},{1,17},{17,1},{2,18},{18,2},{3,19},{19,3},{4,20},{20... | collective-permute-start | bytes 98312 | tf_op jit(solution)/shard_map/ppermute | solution.py:138
  5.1 0.0 copy-start.3
  5.1 0.0 collective-permute-done
  5.2 0.1 collective-permute-done.1
  5.3 0.0 collective-permute-done.2
  5.3 0.5 %copy-done.3 = s32[32,2,2]{0,2,1:T(2,128)S(1)} copy-done((s32[32,2,2]{0,2,1:T(2,128)S(1)}, s32[32,2,2]{0,2,1:T(2,128)}, u32[]{:S(2)}) %copy-start.3) | copy-done | bytes 536
  5.8 0.1 pad_add_fusion
  5.9 3.3 %collective-permute-start.3 = (s32[2,2,128]{2,1,0:T(2,128)S(1)}, s32[2,2,128]{2,1,0:T(2,128)S(1)}, u32[]{:S(2)}, u32[]{:S(2)}) collective-permute-start(s32[2,2,128]{2,1,0:T(2,128)S(1)} %pad_add_fusion), channel_id=1, source_target_pairs={{0,12},{1,13},{2,14},{3,15},{4,8},{5,9},{6,10},{7,11},{8,4},{9,5},... | collective-permute-start | bytes 6152 | tf_op jit(solution)/shard_map/ppermute | solution.py:126
  9.2 0.0 collective-permute-start.4
  9.2 0.4 %collective-permute-start.5 = (s32[2,2,128]{2,1,0:T(2,128)S(1)}, s32[2,2,128]{2,1,0:T(2,128)S(1)}, u32[]{:S(2)}, u32[]{:S(2)}) collective-permute-start(s32[2,2,128]{2,1,0:T(2,128)S(1)} %pad_add_fusion), channel_id=1, source_target_pairs={{0,4},{1,5},{2,6},{3,7},{4,0},{5,1},{6,2},{7,3},{8,12},{9,13},{10,... | collective-permute-start | bytes 6152 | tf_op jit(solution)/shard_map/ppermute | solution.py:126
  9.6 0.0 collective-permute-done.6.refs_5_
  9.6 0.0 copy-done.1
  9.6 0.0 copy-done.2
  9.7 1.4 %collective-permute-start.7 = (bf16[2,2,16,640]{3,2,1,0:T(8,128)(2,1)S(1)}, bf16[2,2,16,640]{3,2,1,0:T(8,128)(2,1)S(1)}, u32[]{:S(2)}, u32[]{:S(2)}) collective-permute-start(bf16[2,2,16,640]{3,2,1,0:T(8,128)(2,1)S(1)} %get-tuple-element.6), channel_id=1, source_target_pairs={{0,1},{1,0},{2,3},{3,2},{4,5},{5,4},{6,7},{7,6},{8,9},{9,8},{10,11... | collective-permute-start | bytes 245768 | tf_op jit(solution)/shard_map/ppermute | solution.py:148
  11.0 3.0 %collective-permute-start.8 = (bf16[2,2,16,640]{3,2,1,0:T(8,128)(2,1)S(1)}, bf16[2,2,16,640]{3,2,1,0:T(8,128)(2,1)S(1)}, u32[]{:S(2)}, u32[]{:S(2)}) collective-permute-start(bf16[2,2,16,640]{3,2,1,0:T(8,128)(2,1)S(1)} %get-tuple-element.5), channel_id=1, source_target_pairs={{1,2},{2,1},{3,4},{4,3},{5,6},{6,5},{7,8},{8,7},{9,10},{10,9},{11,... | collective-permute-start | bytes 245768 | tf_op jit(solution)/shard_map/ppermute | solution.py:150
  14.1 0.0 collective-permute-done.3
  14.1 0.0 collective-permute-done.4
  14.1 0.0 collective-permute-done.5
  14.1 0.1 concatenate.11
  14.2 0.0 copy-start
  14.2 0.0 collective-permute-done.7.refs_3_
  14.2 2.5 %collective-permute-done.8.refs_4_ = bf16[2,2,16,640]{3,2,1,0:T(8,128)(2,1)S(1)} collective-permute-done((bf16[2,2,16,640]{3,2,1,0:T(8,128)(2,1)S(1)}, bf16[2,2,16,640]{3,2,1,0:T(8,128)(2,1)S(1)}, u32[]{:S(2)}, u32[]{:S(2)}) %collective-permute-start.8) | collective-permute-done | bytes 81952 | tf_op jit(solution)/shard_map/ppermute | solution.py:150
  16.8 0.0 copy-done
  16.8 13.6 %search.1 = f32[32,512]{1,0:T(8,128)} custom-call(s32[2048]{0:T(1024)S(1)} %bitcast.5, s32[2,2]{1,0:T(2,128)S(1)} %copy-done, bf16[2,2,32,512]{3,2,1,0:T(8,128)(2,1)S(1)} %pad_maximum_fusion.refs_2_, bf16[2,2,16,640]{3,2,1,0:T(8,128)(2,1)S(1)} %collective-permute-done.7.refs_3_, bf16[2,2,16,640]{3,2,1,0:T(8,128)(2,1)S(1)} %collective-permute-done.8.refs_4_, ...), custom_call_target="tpu_custom_call" | custom-call | tf_op jit(solution)/shard_map/search/pallas_call | solution.py:155
  (4 shorter events, 0.1 us)
Async XLA Ops:
  0.0 5.1 %collective-permute-start = (s32[2,2,32]{2,1,0:T(2,128)}, s32[2,2,32]{2,1,0:T(2,128)S(1)}, u32[]{:S(2)}, u32[]{:S(2)}) collective-permute-start(s32[2,2,32]{2,1,0:T(2,128)} %bitcast.13), channel_id=1, source_target_pairs={{0,3},{1,2},{2,1},{3,0},{4,7},{5,6},{6,5},{7,4},{8,11},{9,10},{10,... | collective-permute-start | bytes 1544 | tf_op jit(solution)/shard_map/ppermute | solution.py:126
  2.6 2.6 %collective-permute-start.1 = (s32[2,2,32]{2,1,0:T(2,128)}, s32[2,2,32]{2,1,0:T(2,128)S(1)}, u32[]{:S(2)}, u32[]{:S(2)}) collective-permute-start(s32[2,2,32]{2,1,0:T(2,128)} %bitcast.14), channel_id=1, source_target_pairs={{0,2},{1,3},{2,0},{3,1},{4,6},{5,7},{6,4},{7,5},{8,10},{9,11},{10,... | collective-permute-start | bytes 1544 | tf_op jit(solution)/shard_map/ppermute | solution.py:126
  2.6 2.6 %collective-permute-start.2 = (s32[2,2,32]{2,1,0:T(2,128)}, s32[2,2,32]{2,1,0:T(2,128)S(1)}, u32[]{:S(2)}, u32[]{:S(2)}) collective-permute-start(s32[2,2,32]{2,1,0:T(2,128)} %bitcast.15), channel_id=1, source_target_pairs={{0,1},{1,0},{2,3},{3,2},{4,5},{5,4},{6,7},{7,6},{8,9},{9,8},{10,11... | collective-permute-start | bytes 1544 | tf_op jit(solution)/shard_map/ppermute | solution.py:126
  3.1 6.5 %copy-start.1 = (bf16[2,32,512]{2,1,0:T(8,128)(2,1)S(1)}, bf16[2,32,512]{2,1,0:T(8,128)(2,1)}, u32[]{:S(2)}) copy-start(bf16[2,32,512]{2,1,0:T(8,128)(2,1)} %param.5) | copy-start | bytes 196612
  3.1 6.5 %copy-start.2 = (bf16[2,32,512]{2,1,0:T(8,128)(2,1)S(1)}, bf16[2,32,512]{2,1,0:T(8,128)(2,1)}, u32[]{:S(2)}) copy-start(bf16[2,32,512]{2,1,0:T(8,128)(2,1)} %param.4) | copy-start | bytes 196612
  3.9 5.7 %collective-permute-start.6 = (bf16[2,2,32,128]{3,2,1,0:T(8,128)(2,1)S(1)}, bf16[2,2,32,128]{3,2,1,0:T(8,128)(2,1)S(1)}, u32[]{:S(2)}, u32[]{:S(2)}) collective-permute-start(bf16[2,2,32,128]{3,2,1,0:T(8,128)(2,1)S(1)} %fusion.1), channel_id=1, source_target_pairs={{0,16},{16,0},{1,17},{17,1},{2,18},{18,2},{3,19},{19,3},{4,20},{20... | collective-permute-start | bytes 98312 | tf_op jit(solution)/shard_map/ppermute | solution.py:138
  5.1 0.7 %copy-start.3 = (s32[32,2,2]{0,2,1:T(2,128)S(1)}, s32[32,2,2]{0,2,1:T(2,128)}, u32[]{:S(2)}) copy-start(s32[32,2,2]{0,2,1:T(2,128)} %param.6) | copy-start | bytes 1540
  5.9 8.2 %collective-permute-start.3 = (s32[2,2,128]{2,1,0:T(2,128)S(1)}, s32[2,2,128]{2,1,0:T(2,128)S(1)}, u32[]{:S(2)}, u32[]{:S(2)}) collective-permute-start(s32[2,2,128]{2,1,0:T(2,128)S(1)} %pad_add_fusion), channel_id=1, source_target_pairs={{0,12},{1,13},{2,14},{3,15},{4,8},{5,9},{6,10},{7,11},{8,4},{9,5},... | collective-permute-start | bytes 6152 | tf_op jit(solution)/shard_map/ppermute | solution.py:126
  9.2 4.9 %collective-permute-start.4 = (s32[2,2,128]{2,1,0:T(2,128)S(1)}, s32[2,2,128]{2,1,0:T(2,128)S(1)}, u32[]{:S(2)}, u32[]{:S(2)}) collective-permute-start(s32[2,2,128]{2,1,0:T(2,128)S(1)} %pad_add_fusion), channel_id=1, source_target_pairs={{0,8},{1,9},{2,10},{3,11},{4,12},{5,13},{6,14},{7,15},{8,0},{9,1},... | collective-permute-start | bytes 6152 | tf_op jit(solution)/shard_map/ppermute | solution.py:126
  9.2 4.9 %collective-permute-start.5 = (s32[2,2,128]{2,1,0:T(2,128)S(1)}, s32[2,2,128]{2,1,0:T(2,128)S(1)}, u32[]{:S(2)}, u32[]{:S(2)}) collective-permute-start(s32[2,2,128]{2,1,0:T(2,128)S(1)} %pad_add_fusion), channel_id=1, source_target_pairs={{0,4},{1,5},{2,6},{3,7},{4,0},{5,1},{6,2},{7,3},{8,12},{9,13},{10,... | collective-permute-start | bytes 6152 | tf_op jit(solution)/shard_map/ppermute | solution.py:126
  9.7 4.6 %collective-permute-start.7 = (bf16[2,2,16,640]{3,2,1,0:T(8,128)(2,1)S(1)}, bf16[2,2,16,640]{3,2,1,0:T(8,128)(2,1)S(1)}, u32[]{:S(2)}, u32[]{:S(2)}) collective-permute-start(bf16[2,2,16,640]{3,2,1,0:T(8,128)(2,1)S(1)} %get-tuple-element.6), channel_id=1, source_target_pairs={{0,1},{1,0},{2,3},{3,2},{4,5},{5,4},{6,7},{7,6},{8,9},{9,8},{10,11... | collective-permute-start | bytes 245768 | tf_op jit(solution)/shard_map/ppermute | solution.py:148
  11.0 5.7 %collective-permute-start.8 = (bf16[2,2,16,640]{3,2,1,0:T(8,128)(2,1)S(1)}, bf16[2,2,16,640]{3,2,1,0:T(8,128)(2,1)S(1)}, u32[]{:S(2)}, u32[]{:S(2)}) collective-permute-start(bf16[2,2,16,640]{3,2,1,0:T(8,128)(2,1)S(1)} %get-tuple-element.5), channel_id=1, source_target_pairs={{1,2},{2,1},{3,4},{4,3},{5,6},{6,5},{7,8},{8,7},{9,10},{10,9},{11,... | collective-permute-start | bytes 245768 | tf_op jit(solution)/shard_map/ppermute | solution.py:150
  14.2 2.5 %copy-start = (s32[2,2]{1,0:T(2,128)S(1)}, s32[2,2]{1,0:T(2,128)}, u32[]{:S(2)}) copy-start(s32[2,2]{1,0:T(2,128)} %refs_1_.1) | copy-start | bytes 52

commit v5 on v4

--- a/solution.py
+++ b/solution.py
@@ -14,7 +14,9 @@
 
 
 def search_kernel(n_sky, height, breadth, epochs, *refs):
-    table, mask_ref, own_ref, near_ref, far_ref, *side_refs, best_ref, pairs, copies = refs
+    table_in, mask_ref, own_ref, near_ref, far_ref, *side_refs, best_ref, pairs, copies, table, arrived = refs
+    table_copy = pltpu.make_async_copy(table_in, table, arrived)
+    table_copy.start()
     spots = 2 * MAXS + 1
     rows = height + 2 * MAXS
     tiles = breadth // LANES
@@ -91,17 +93,27 @@
         for epoch in range(epochs):
             down, across = table[2 * epoch * count + index], table[(2 * epoch + 1) * count + index]
             bases.append((across + MAXS) * (tiles * depth) + down + (MAXS + epoch * 2 * rows))
-        out = []
+        out, waiting = list(best), []
+
+        def finish():
+            part, psi_sum, scale = waiting.pop(0)
+            out[part] = jnp.maximum(out[part], psi_sum * scale)
+
         for part in range(len(best)):
             at = part // row_tiles * depth + part % row_tiles * SUBLANES
             psi_sum = functools.reduce(operator.add, [copies[pl.ds(base + at, SUBLANES), :] for base in bases])
             phi_sum = functools.reduce(operator.add, [copies[pl.ds(base + (at + rows), SUBLANES), :] for base in bases])
-            out.append(jnp.maximum(best[part], psi_sum * lax.rsqrt(jnp.maximum(phi_sum, 1.0))))
+            waiting.append((part, psi_sum, lax.rsqrt(jnp.maximum(phi_sum, 1.0))))
+            if len(waiting) > 3:
+                finish()
+        while waiting:
+            finish()
         return tuple(out)
 
     row_tiles = height // SUBLANES
     best = tuple(jnp.full((SUBLANES, LANES), -1e30, jnp.float32) for _ in range(tiles * row_tiles))
     unroll = 4
+    table_copy.wait()
     count = table.shape[0] // (2 * epochs)
 
     def steps(step, best):
@@ -155,11 +167,13 @@
     return pl.pallas_call(
         functools.partial(search_kernel, n_sky, height, breadth, epochs),
         out_shape=jax.ShapeDtypeStruct((height, breadth), jnp.float32),
-        in_specs=[smem] * 2 + [vmem] * (3 + len(sides)),
+        in_specs=[vmem, smem] + [vmem] * (3 + len(sides)),
         out_specs=vmem,
         scratch_shapes=[
             pltpu.VMEM((breadth // LANES + 1, epochs * 2 * rows, 2 * LANES), jnp.bfloat16),
             pltpu.VMEM((slabs * rows, LANES), jnp.float32),
+            pltpu.SMEM(table.shape, jnp.int32),
+            pltpu.SemaphoreType.DMA(()),
         ],
         compiler_params=pltpu.CompilerParams(vmem_limit_bytes=40 * 2**20),
         name="search",

time: 30.6 us -> 30.4 us (level)
  no operation moved by 1% of the time
where the time goes in v5:
time: 30.4 us; the launch traced here: 30.1 us
  Pallas kernels  13.3 us (44%)
  starting transfers between devices  12.4 us (41%)
  waiting for transfers between devices  2.66 us (9%)
  other arithmetic  0.94 us (3%)
  local copies, waits for them, and re-layouts  0.66 us (2%)
    pallas_call x1, Pallas kernels, body(): pl.pallas_call(functools.partial(search_kernel, n_sky, height, breadth, e...  13.3 us
    ppermute x6, starting transfers between devices, gathered(): lax.ppermute(held, axis, [(i, i ^ turn * stride) for i in range(count)])  6.75 us
    ppermute x1, starting transfers between devices, body(): far = lax.ppermute(jnp.where(even, top, bottom), 'vel', others)  3.05 us
    ppermute x1, waiting for transfers between devices, body(): far = lax.ppermute(jnp.where(even, top, bottom), 'vel', others)  2.52 us
    ppermute x1, starting transfers between devices, body(): lax.ppermute(jnp.where(even, bottom, top), 'vel', [(i, i ^ 1) for i in ra...  1.36 us
    ppermute x1, starting transfers between devices, body(): sides = [lax.ppermute(edge, 'sky', [(0, 1), (1, 0)])]  1.27 us
    select_n x1, other arithmetic, body(): edge = jnp.where(lax.axis_index('sky') == 0, last, first)  0.81 us
  transfers between devices with their start and end apart: 9, of which 2 were waited for; matrix products, arithmetic and copies ran while one was open for 3% of the time, Pallas kernels for 0%

profile of v5, /device:TPU:1, one launch (start us, length us, event | category | flops | bytes accessed | tf_op | source)
XLA Modules:
  0.0 30.1 jit_solution(4820436115606159536)
XLA Ops:
  0.0 2.6 %collective-permute-start = (s32[2,2,32]{2,1,0:T(2,128)}, s32[2,2,32]{2,1,0:T(2,128)S(1)}, u32[]{:S(2)}, u32[]{:S(2)}) collective-permute-start(s32[2,2,32]{2,1,0:T(2,128)} %bitcast.13), channel_id=1, source_target_pairs={{0,3},{1,2},{2,1},{3,0},{4,7},{5,6},{6,5},{7,4},{8,11},{9,10},{10,... | collective-permute-start | bytes 1544 | tf_op jit(solution)/shard_map/ppermute | solution.py:138
  2.6 0.0 collective-permute-start.1
  2.6 0.4 %collective-permute-start.2 = (s32[2,2,32]{2,1,0:T(2,128)}, s32[2,2,32]{2,1,0:T(2,128)S(1)}, u32[]{:S(2)}, u32[]{:S(2)}) collective-permute-start(s32[2,2,32]{2,1,0:T(2,128)} %bitcast.15), channel_id=1, source_target_pairs={{0,1},{1,0},{2,3},{3,2},{4,5},{5,4},{6,7},{7,6},{8,9},{9,8},{10,11... | collective-permute-start | bytes 1544 | tf_op jit(solution)/shard_map/ppermute | solution.py:138
  3.1 0.0 copy-start.1
  3.1 0.0 copy-start.2
  3.1 0.8 %fusion.1 = bf16[2,2,32,128]{3,2,1,0:T(8,128)(2,1)S(1)} fusion(bf16[2,1,32,512]{3,2,1,0:T(8,128)(2,1)} %bitcast.9, bf16[2,1,32,512]{3,2,1,0:T(8,128)(2,1)} %bitcast.6, pred[]{:T(512)S(6)} %eq.7), kind=kLoop, calls=%fused_computation.9 | loop fusion | flops 49152 | bytes 163841 | tf_op jit(solution)/shard_map/jit(_where)/select_n | solution.py:149
  3.9 1.3 %collective-permute-start.6 = (bf16[2,2,32,128]{3,2,1,0:T(8,128)(2,1)S(1)}, bf16[2,2,32,128]{3,2,1,0:T(8,128)(2,1)S(1)}, u32[]{:S(2)}, u32[]{:S(2)}) collective-permute-start(bf16[2,2,32,128]{3,2,1,0:T(8,128)(2,1)S(1)} %fusion.1), channel_id=1, source_target_pairs={{0,16},{16,0},{1,17},{17,1},{2,18},{18,2},{3,19},{19,3},{4,20},{20... | collective-permute-start | bytes 98312 | tf_op jit(solution)/shard_map/ppermute | solution.py:150
  5.1 0.0 copy-start.3
  5.1 0.0 collective-permute-done
  5.2 0.1 collective-permute-done.1
  5.3 0.0 collective-permute-done.2
  5.3 0.5 %copy-done.3 = s32[32,2,2]{0,2,1:T(2,128)S(1)} copy-done((s32[32,2,2]{0,2,1:T(2,128)S(1)}, s32[32,2,2]{0,2,1:T(2,128)}, u32[]{:S(2)}) %copy-start.3) | copy-done | bytes 536
  5.8 0.1 pad_add_fusion
  5.9 3.3 %collective-permute-start.3 = (s32[2,2,128]{2,1,0:T(2,128)S(1)}, s32[2,2,128]{2,1,0:T(2,128)S(1)}, u32[]{:S(2)}, u32[]{:S(2)}) collective-permute-start(s32[2,2,128]{2,1,0:T(2,128)S(1)} %pad_add_fusion), channel_id=1, source_target_pairs={{0,12},{1,13},{2,14},{3,15},{4,8},{5,9},{6,10},{7,11},{8,4},{9,5},... | collective-permute-start | bytes 6152 | tf_op jit(solution)/shard_map/ppermute | solution.py:138
  9.2 0.0 collective-permute-start.4
  9.2 0.4 %collective-permute-start.5 = (s32[2,2,128]{2,1,0:T(2,128)S(1)}, s32[2,2,128]{2,1,0:T(2,128)S(1)}, u32[]{:S(2)}, u32[]{:S(2)}) collective-permute-start(s32[2,2,128]{2,1,0:T(2,128)S(1)} %pad_add_fusion), channel_id=1, source_target_pairs={{0,4},{1,5},{2,6},{3,7},{4,0},{5,1},{6,2},{7,3},{8,12},{9,13},{10,... | collective-permute-start | bytes 6152 | tf_op jit(solution)/shard_map/ppermute | solution.py:138
  9.6 0.0 collective-permute-done.6.refs_5_
  9.6 0.0 copy-done.1
  9.6 0.0 copy-done.2
  9.7 1.4 %collective-permute-start.7 = (bf16[2,2,16,640]{3,2,1,0:T(8,128)(2,1)S(1)}, bf16[2,2,16,640]{3,2,1,0:T(8,128)(2,1)S(1)}, u32[]{:S(2)}, u32[]{:S(2)}) collective-permute-start(bf16[2,2,16,640]{3,2,1,0:T(8,128)(2,1)S(1)} %get-tuple-element.6), channel_id=1, source_target_pairs={{0,1},{1,0},{2,3},{3,2},{4,5},{5,4},{6,7},{7,6},{8,9},{9,8},{10,11... | collective-permute-start | bytes 245768 | tf_op jit(solution)/shard_map/ppermute | solution.py:160
  11.0 3.0 %collective-permute-start.8 = (bf16[2,2,16,640]{3,2,1,0:T(8,128)(2,1)S(1)}, bf16[2,2,16,640]{3,2,1,0:T(8,128)(2,1)S(1)}, u32[]{:S(2)}, u32[]{:S(2)}) collective-permute-start(bf16[2,2,16,640]{3,2,1,0:T(8,128)(2,1)S(1)} %get-tuple-element.5), channel_id=1, source_target_pairs={{1,2},{2,1},{3,4},{4,3},{5,6},{6,5},{7,8},{8,7},{9,10},{10,9},{11,... | collective-permute-start | bytes 245768 | tf_op jit(solution)/shard_map/ppermute | solution.py:162
  14.1 0.0 collective-permute-done.3
  14.1 0.0 collective-permute-done.4
  14.1 0.0 collective-permute-done.5
  14.1 0.1 concatenate.11
  14.2 0.0 copy-start
  14.2 0.0 collective-permute-done.7.refs_3_
  14.2 2.5 %collective-permute-done.8.refs_4_ = bf16[2,2,16,640]{3,2,1,0:T(8,128)(2,1)S(1)} collective-permute-done((bf16[2,2,16,640]{3,2,1,0:T(8,128)(2,1)S(1)}, bf16[2,2,16,640]{3,2,1,0:T(8,128)(2,1)S(1)}, u32[]{:S(2)}, u32[]{:S(2)}) %collective-permute-start.8) | collective-permute-done | bytes 81952 | tf_op jit(solution)/shard_map/ppermute | solution.py:162
  16.8 0.0 copy-done
  16.8 13.3 %search.1 = f32[32,512]{1,0:T(8,128)} custom-call(s32[2048]{0:T(1024)S(1)} %bitcast.5, s32[2,2]{1,0:T(2,128)S(1)} %copy-done, bf16[2,2,32,512]{3,2,1,0:T(8,128)(2,1)S(1)} %pad_maximum_fusion.refs_2_, bf16[2,2,16,640]{3,2,1,0:T(8,128)(2,1)S(1)} %collective-permute-done.7.refs_3_, bf16[2,2,16,640]{3,2,1,0:T(8,128)(2,1)S(1)} %collective-permute-done.8.refs_4_, ...), custom_call_target="tpu_custom_call" | custom-call | tf_op jit(solution)/shard_map/search/pallas_call | solution.py:167
  (4 shorter events, 0.1 us)
Async XLA Ops:
  0.0 5.1 %collective-permute-start = (s32[2,2,32]{2,1,0:T(2,128)}, s32[2,2,32]{2,1,0:T(2,128)S(1)}, u32[]{:S(2)}, u32[]{:S(2)}) collective-permute-start(s32[2,2,32]{2,1,0:T(2,128)} %bitcast.13), channel_id=1, source_target_pairs={{0,3},{1,2},{2,1},{3,0},{4,7},{5,6},{6,5},{7,4},{8,11},{9,10},{10,... | collective-permute-start | bytes 1544 | tf_op jit(solution)/shard_map/ppermute | solution.py:138
  2.6 2.6 %collective-permute-start.1 = (s32[2,2,32]{2,1,0:T(2,128)}, s32[2,2,32]{2,1,0:T(2,128)S(1)}, u32[]{:S(2)}, u32[]{:S(2)}) collective-permute-start(s32[2,2,32]{2,1,0:T(2,128)} %bitcast.14), channel_id=1, source_target_pairs={{0,2},{1,3},{2,0},{3,1},{4,6},{5,7},{6,4},{7,5},{8,10},{9,11},{10,... | collective-permute-start | bytes 1544 | tf_op jit(solution)/shard_map/ppermute | solution.py:138
  2.6 2.6 %collective-permute-start.2 = (s32[2,2,32]{2,1,0:T(2,128)}, s32[2,2,32]{2,1,0:T(2,128)S(1)}, u32[]{:S(2)}, u32[]{:S(2)}) collective-permute-start(s32[2,2,32]{2,1,0:T(2,128)} %bitcast.15), channel_id=1, source_target_pairs={{0,1},{1,0},{2,3},{3,2},{4,5},{5,4},{6,7},{7,6},{8,9},{9,8},{10,11... | collective-permute-start | bytes 1544 | tf_op jit(solution)/shard_map/ppermute | solution.py:138
  3.1 6.5 %copy-start.1 = (bf16[2,32,512]{2,1,0:T(8,128)(2,1)S(1)}, bf16[2,32,512]{2,1,0:T(8,128)(2,1)}, u32[]{:S(2)}) copy-start(bf16[2,32,512]{2,1,0:T(8,128)(2,1)} %param.5) | copy-start | bytes 196612
  3.1 6.5 %copy-start.2 = (bf16[2,32,512]{2,1,0:T(8,128)(2,1)S(1)}, bf16[2,32,512]{2,1,0:T(8,128)(2,1)}, u32[]{:S(2)}) copy-start(bf16[2,32,512]{2,1,0:T(8,128)(2,1)} %param.4) | copy-start | bytes 196612
  3.9 5.7 %collective-permute-start.6 = (bf16[2,2,32,128]{3,2,1,0:T(8,128)(2,1)S(1)}, bf16[2,2,32,128]{3,2,1,0:T(8,128)(2,1)S(1)}, u32[]{:S(2)}, u32[]{:S(2)}) collective-permute-start(bf16[2,2,32,128]{3,2,1,0:T(8,128)(2,1)S(1)} %fusion.1), channel_id=1, source_target_pairs={{0,16},{16,0},{1,17},{17,1},{2,18},{18,2},{3,19},{19,3},{4,20},{20... | collective-permute-start | bytes 98312 | tf_op jit(solution)/shard_map/ppermute | solution.py:150
  5.1 0.7 %copy-start.3 = (s32[32,2,2]{0,2,1:T(2,128)S(1)}, s32[32,2,2]{0,2,1:T(2,128)}, u32[]{:S(2)}) copy-start(s32[32,2,2]{0,2,1:T(2,128)} %param.6) | copy-start | bytes 1540
  5.9 8.2 %collective-permute-start.3 = (s32[2,2,128]{2,1,0:T(2,128)S(1)}, s32[2,2,128]{2,1,0:T(2,128)S(1)}, u32[]{:S(2)}, u32[]{:S(2)}) collective-permute-start(s32[2,2,128]{2,1,0:T(2,128)S(1)} %pad_add_fusion), channel_id=1, source_target_pairs={{0,12},{1,13},{2,14},{3,15},{4,8},{5,9},{6,10},{7,11},{8,4},{9,5},... | collective-permute-start | bytes 6152 | tf_op jit(solution)/shard_map/ppermute | solution.py:138
  9.2 4.9 %collective-permute-start.4 = (s32[2,2,128]{2,1,0:T(2,128)S(1)}, s32[2,2,128]{2,1,0:T(2,128)S(1)}, u32[]{:S(2)}, u32[]{:S(2)}) collective-permute-start(s32[2,2,128]{2,1,0:T(2,128)S(1)} %pad_add_fusion), channel_id=1, source_target_pairs={{0,8},{1,9},{2,10},{3,11},{4,12},{5,13},{6,14},{7,15},{8,0},{9,1},... | collective-permute-start | bytes 6152 | tf_op jit(solution)/shard_map/ppermute | solution.py:138
  9.2 4.9 %collective-permute-start.5 = (s32[2,2,128]{2,1,0:T(2,128)S(1)}, s32[2,2,128]{2,1,0:T(2,128)S(1)}, u32[]{:S(2)}, u32[]{:S(2)}) collective-permute-start(s32[2,2,128]{2,1,0:T(2,128)S(1)} %pad_add_fusion), channel_id=1, source_target_pairs={{0,4},{1,5},{2,6},{3,7},{4,0},{5,1},{6,2},{7,3},{8,12},{9,13},{10,... | collective-permute-start | bytes 6152 | tf_op jit(solution)/shard_map/ppermute | solution.py:138
  9.7 4.6 %collective-permute-start.7 = (bf16[2,2,16,640]{3,2,1,0:T(8,128)(2,1)S(1)}, bf16[2,2,16,640]{3,2,1,0:T(8,128)(2,1)S(1)}, u32[]{:S(2)}, u32[]{:S(2)}) collective-permute-start(bf16[2,2,16,640]{3,2,1,0:T(8,128)(2,1)S(1)} %get-tuple-element.6), channel_id=1, source_target_pairs={{0,1},{1,0},{2,3},{3,2},{4,5},{5,4},{6,7},{7,6},{8,9},{9,8},{10,11... | collective-permute-start | bytes 245768 | tf_op jit(solution)/shard_map/ppermute | solution.py:160
  11.0 5.7 %collective-permute-start.8 = (bf16[2,2,16,640]{3,2,1,0:T(8,128)(2,1)S(1)}, bf16[2,2,16,640]{3,2,1,0:T(8,128)(2,1)S(1)}, u32[]{:S(2)}, u32[]{:S(2)}) collective-permute-start(bf16[2,2,16,640]{3,2,1,0:T(8,128)(2,1)S(1)} %get-tuple-element.5), channel_id=1, source_target_pairs={{1,2},{2,1},{3,4},{4,3},{5,6},{6,5},{7,8},{8,7},{9,10},{10,9},{11,... | collective-permute-start | bytes 245768 | tf_op jit(solution)/shard_map/ppermute | solution.py:162
  14.2 2.5 %copy-start = (s32[2,2]{1,0:T(2,128)S(1)}, s32[2,2]{1,0:T(2,128)}, u32[]{:S(2)}) copy-start(s32[2,2]{1,0:T(2,128)} %refs_1_.1) | copy-start | bytes 52

commit v6 on v5

--- a/solution.py
+++ b/solution.py
@@ -134,7 +134,7 @@
         radix = 4 if count // stride % 4 == 0 else 2
         held = jnp.concatenate(parts, axis=-1) if len(parts) > 1 else piece
         parts = [held]
-        for turn in range(radix - 1, 0, -1):
+        for turn in (3, 2, 1) if stride == 1 and radix == 4 else (2, 3, 1) if radix == 4 else (1,):
             parts.append(lax.ppermute(held, axis, [(i, i ^ (turn * stride)) for i in range(count)]))
         stride *= radix
     return jnp.concatenate(parts, axis=-1).reshape(-1)

time: 30.4 us -> 30.4 us (level)
  no operation moved by 1% of the time
where the time goes in v6:
time: 30.4 us; the launch traced here: 29.9 us
  Pallas kernels  13.4 us (44%)
  starting transfers between devices  12.2 us (40%)
  waiting for transfers between devices  2.66 us (9%)
  other arithmetic  0.94 us (3%)
  local copies, waits for them, and re-layouts  0.66 us (2%)
    pallas_call x1, Pallas kernels, body(): pl.pallas_call(functools.partial(search_kernel, n_sky, height, breadth, e...  13.4 us
    ppermute x6, starting transfers between devices, gathered(): lax.ppermute(held, axis, [(i, i ^ turn * stride) for i in range(count)])  6.67 us
    ppermute x1, starting transfers between devices, body(): far = lax.ppermute(jnp.where(even, top, bottom), 'vel', others)  3.05 us
    ppermute x1, waiting for transfers between devices, body(): far = lax.ppermute(jnp.where(even, top, bottom), 'vel', others)  2.52 us
    ppermute x1, starting transfers between devices, body(): sides = [lax.ppermute(edge, 'sky', [(0, 1), (1, 0)])]  1.27 us
    ppermute x1, starting transfers between devices, body(): lax.ppermute(jnp.where(even, bottom, top), 'vel', [(i, i ^ 1) for i in ra...  1.21 us
    select_n x1, other arithmetic, body(): edge = jnp.where(lax.axis_index('sky') == 0, last, first)  0.81 us
  transfers between devices with their start and end apart: 9, of which 2 were waited for; matrix products, arithmetic and copies ran while one was open for 3% of the time, Pallas kernels for 0%

profile of v6, /device:TPU:1, one launch (start us, length us, event | category | flops | bytes accessed | tf_op | source)
XLA Modules:
  0.0 29.9 jit_solution(5662517389033817349)
XLA Ops:
  0.0 2.6 %collective-permute-start = (s32[2,2,32]{2,1,0:T(2,128)}, s32[2,2,32]{2,1,0:T(2,128)S(1)}, u32[]{:S(2)}, u32[]{:S(2)}) collective-permute-start(s32[2,2,32]{2,1,0:T(2,128)} %bitcast.13), channel_id=1, source_target_pairs={{0,3},{1,2},{2,1},{3,0},{4,7},{5,6},{6,5},{7,4},{8,11},{9,10},{10,... | collective-permute-start | bytes 1544 | tf_op jit(solution)/shard_map/ppermute | solution.py:138
  2.6 0.0 collective-permute-start.1
  2.6 0.4 %collective-permute-start.2 = (s32[2,2,32]{2,1,0:T(2,128)}, s32[2,2,32]{2,1,0:T(2,128)S(1)}, u32[]{:S(2)}, u32[]{:S(2)}) collective-permute-start(s32[2,2,32]{2,1,0:T(2,128)} %bitcast.15), channel_id=1, source_target_pairs={{0,1},{1,0},{2,3},{3,2},{4,5},{5,4},{6,7},{7,6},{8,9},{9,8},{10,11... | collective-permute-start | bytes 1544 | tf_op jit(solution)/shard_map/ppermute | solution.py:138
  3.1 0.0 copy-start.1
  3.1 0.0 copy-start.2
  3.1 0.8 %fusion.1 = bf16[2,2,32,128]{3,2,1,0:T(8,128)(2,1)S(1)} fusion(bf16[2,1,32,512]{3,2,1,0:T(8,128)(2,1)} %bitcast.9, bf16[2,1,32,512]{3,2,1,0:T(8,128)(2,1)} %bitcast.6, pred[]{:T(512)S(6)} %eq.7), kind=kLoop, calls=%fused_computation.9 | loop fusion | flops 49152 | bytes 163841 | tf_op jit(solution)/shard_map/jit(_where)/select_n | solution.py:149
  3.9 1.3 %collective-permute-start.6 = (bf16[2,2,32,128]{3,2,1,0:T(8,128)(2,1)S(1)}, bf16[2,2,32,128]{3,2,1,0:T(8,128)(2,1)S(1)}, u32[]{:S(2)}, u32[]{:S(2)}) collective-permute-start(bf16[2,2,32,128]{3,2,1,0:T(8,128)(2,1)S(1)} %fusion.1), channel_id=1, source_target_pairs={{0,16},{16,0},{1,17},{17,1},{2,18},{18,2},{3,19},{19,3},{4,20},{20... | collective-permute-start | bytes 98312 | tf_op jit(solution)/shard_map/ppermute | solution.py:150
  5.1 0.0 copy-start.3
  5.1 0.0 collective-permute-done
  5.2 0.1 collective-permute-done.1
  5.3 0.0 collective-permute-done.2
  5.3 0.5 %copy-done.3 = s32[32,2,2]{0,2,1:T(2,128)S(1)} copy-done((s32[32,2,2]{0,2,1:T(2,128)S(1)}, s32[32,2,2]{0,2,1:T(2,128)}, u32[]{:S(2)}) %copy-start.3) | copy-done | bytes 536
  5.8 0.1 pad_add_fusion
  5.9 2.3 %collective-permute-start.3 = (s32[2,2,128]{2,1,0:T(2,128)S(1)}, s32[2,2,128]{2,1,0:T(2,128)S(1)}, u32[]{:S(2)}, u32[]{:S(2)}) collective-permute-start(s32[2,2,128]{2,1,0:T(2,128)S(1)} %pad_add_fusion), channel_id=1, source_target_pairs={{0,8},{1,9},{2,10},{3,11},{4,12},{5,13},{6,14},{7,15},{8,0},{9,1},... | collective-permute-start | bytes 6152 | tf_op jit(solution)/shard_map/ppermute | solution.py:138
  8.2 1.1 %collective-permute-start.4 = (s32[2,2,128]{2,1,0:T(2,128)S(1)}, s32[2,2,128]{2,1,0:T(2,128)S(1)}, u32[]{:S(2)}, u32[]{:S(2)}) collective-permute-start(s32[2,2,128]{2,1,0:T(2,128)S(1)} %pad_add_fusion), channel_id=1, source_target_pairs={{0,12},{1,13},{2,14},{3,15},{4,8},{5,9},{6,10},{7,11},{8,4},{9,5},... | collective-permute-start | bytes 6152 | tf_op jit(solution)/shard_map/ppermute | solution.py:138
  9.3 0.2 collective-permute-start.5
  9.5 0.0 collective-permute-done.6.refs_5_
  9.5 0.0 copy-done.1
  9.5 0.0 copy-done.2
  9.6 1.2 %collective-permute-start.7 = (bf16[2,2,16,640]{3,2,1,0:T(8,128)(2,1)S(1)}, bf16[2,2,16,640]{3,2,1,0:T(8,128)(2,1)S(1)}, u32[]{:S(2)}, u32[]{:S(2)}) collective-permute-start(bf16[2,2,16,640]{3,2,1,0:T(8,128)(2,1)S(1)} %get-tuple-element.6), channel_id=1, source_target_pairs={{0,1},{1,0},{2,3},{3,2},{4,5},{5,4},{6,7},{7,6},{8,9},{9,8},{10,11... | collective-permute-start | bytes 245768 | tf_op jit(solution)/shard_map/ppermute | solution.py:160
  10.8 3.0 %collective-permute-start.8 = (bf16[2,2,16,640]{3,2,1,0:T(8,128)(2,1)S(1)}, bf16[2,2,16,640]{3,2,1,0:T(8,128)(2,1)S(1)}, u32[]{:S(2)}, u32[]{:S(2)}) collective-permute-start(bf16[2,2,16,640]{3,2,1,0:T(8,128)(2,1)S(1)} %get-tuple-element.5), channel_id=1, source_target_pairs={{1,2},{2,1},{3,4},{4,3},{5,6},{6,5},{7,8},{8,7},{9,10},{10,9},{11,... | collective-permute-start | bytes 245768 | tf_op jit(solution)/shard_map/ppermute | solution.py:162
  13.9 0.0 collective-permute-done.3
  13.9 0.0 collective-permute-done.4
  13.9 0.0 collective-permute-done.5
  13.9 0.1 concatenate.11
  14.0 0.0 copy-start
  14.0 0.0 collective-permute-done.7.refs_3_
  14.0 2.5 %collective-permute-done.8.refs_4_ = bf16[2,2,16,640]{3,2,1,0:T(8,128)(2,1)S(1)} collective-permute-done((bf16[2,2,16,640]{3,2,1,0:T(8,128)(2,1)S(1)}, bf16[2,2,16,640]{3,2,1,0:T(8,128)(2,1)S(1)}, u32[]{:S(2)}, u32[]{:S(2)}) %collective-permute-start.8) | collective-permute-done | bytes 81952 | tf_op jit(solution)/shard_map/ppermute | solution.py:162
  16.5 0.0 copy-done
  16.5 13.4 %search.1 = f32[32,512]{1,0:T(8,128)} custom-call(s32[2048]{0:T(1024)S(1)} %bitcast.5, s32[2,2]{1,0:T(2,128)S(1)} %copy-done, bf16[2,2,32,512]{3,2,1,0:T(8,128)(2,1)S(1)} %pad_maximum_fusion.refs_2_, bf16[2,2,16,640]{3,2,1,0:T(8,128)(2,1)S(1)} %collective-permute-done.7.refs_3_, bf16[2,2,16,640]{3,2,1,0:T(8,128)(2,1)S(1)} %collective-permute-done.8.refs_4_, ...), custom_call_target="tpu_custom_call" | custom-call | tf_op jit(solution)/shard_map/search/pallas_call | solution.py:167
  (4 shorter events, 0.1 us)
Async XLA Ops:
  0.0 5.1 %collective-permute-start = (s32[2,2,32]{2,1,0:T(2,128)}, s32[2,2,32]{2,1,0:T(2,128)S(1)}, u32[]{:S(2)}, u32[]{:S(2)}) collective-permute-start(s32[2,2,32]{2,1,0:T(2,128)} %bitcast.13), channel_id=1, source_target_pairs={{0,3},{1,2},{2,1},{3,0},{4,7},{5,6},{6,5},{7,4},{8,11},{9,10},{10,... | collective-permute-start | bytes 1544 | tf_op jit(solution)/shard_map/ppermute | solution.py:138
  2.6 2.6 %collective-permute-start.1 = (s32[2,2,32]{2,1,0:T(2,128)}, s32[2,2,32]{2,1,0:T(2,128)S(1)}, u32[]{:S(2)}, u32[]{:S(2)}) collective-permute-start(s32[2,2,32]{2,1,0:T(2,128)} %bitcast.14), channel_id=1, source_target_pairs={{0,2},{1,3},{2,0},{3,1},{4,6},{5,7},{6,4},{7,5},{8,10},{9,11},{10,... | collective-permute-start | bytes 1544 | tf_op jit(solution)/shard_map/ppermute | solution.py:138
  2.6 2.6 %collective-permute-start.2 = (s32[2,2,32]{2,1,0:T(2,128)}, s32[2,2,32]{2,1,0:T(2,128)S(1)}, u32[]{:S(2)}, u32[]{:S(2)}) collective-permute-start(s32[2,2,32]{2,1,0:T(2,128)} %bitcast.15), channel_id=1, source_target_pairs={{0,1},{1,0},{2,3},{3,2},{4,5},{5,4},{6,7},{7,6},{8,9},{9,8},{10,11... | collective-permute-start | bytes 1544 | tf_op jit(solution)/shard_map/ppermute | solution.py:138
  3.1 6.5 %copy-start.1 = (bf16[2,32,512]{2,1,0:T(8,128)(2,1)S(1)}, bf16[2,32,512]{2,1,0:T(8,128)(2,1)}, u32[]{:S(2)}) copy-start(bf16[2,32,512]{2,1,0:T(8,128)(2,1)} %param.5) | copy-start | bytes 196612
  3.1 6.5 %copy-start.2 = (bf16[2,32,512]{2,1,0:T(8,128)(2,1)S(1)}, bf16[2,32,512]{2,1,0:T(8,128)(2,1)}, u32[]{:S(2)}) copy-start(bf16[2,32,512]{2,1,0:T(8,128)(2,1)} %param.4) | copy-start | bytes 196612
  3.9 5.6 %collective-permute-start.6 = (bf16[2,2,32,128]{3,2,1,0:T(8,128)(2,1)S(1)}, bf16[2,2,32,128]{3,2,1,0:T(8,128)(2,1)S(1)}, u32[]{:S(2)}, u32[]{:S(2)}) collective-permute-start(bf16[2,2,32,128]{3,2,1,0:T(8,128)(2,1)S(1)} %fusion.1), channel_id=1, source_target_pairs={{0,16},{16,0},{1,17},{17,1},{2,18},{18,2},{3,19},{19,3},{4,20},{20... | collective-permute-start | bytes 98312 | tf_op jit(solution)/shard_map/ppermute | solution.py:150
  5.1 0.7 %copy-start.3 = (s32[32,2,2]{0,2,1:T(2,128)S(1)}, s32[32,2,2]{0,2,1:T(2,128)}, u32[]{:S(2)}) copy-start(s32[32,2,2]{0,2,1:T(2,128)} %param.6) | copy-start | bytes 1540
  5.9 8.0 %collective-permute-start.3 = (s32[2,2,128]{2,1,0:T(2,128)S(1)}, s32[2,2,128]{2,1,0:T(2,128)S(1)}, u32[]{:S(2)}, u32[]{:S(2)}) collective-permute-start(s32[2,2,128]{2,1,0:T(2,128)S(1)} %pad_add_fusion), channel_id=1, source_target_pairs={{0,8},{1,9},{2,10},{3,11},{4,12},{5,13},{6,14},{7,15},{8,0},{9,1},... | collective-permute-start | bytes 6152 | tf_op jit(solution)/shard_map/ppermute | solution.py:138
  8.2 5.7 %collective-permute-start.4 = (s32[2,2,128]{2,1,0:T(2,128)S(1)}, s32[2,2,128]{2,1,0:T(2,128)S(1)}, u32[]{:S(2)}, u32[]{:S(2)}) collective-permute-start(s32[2,2,128]{2,1,0:T(2,128)S(1)} %pad_add_fusion), channel_id=1, source_target_pairs={{0,12},{1,13},{2,14},{3,15},{4,8},{5,9},{6,10},{7,11},{8,4},{9,5},... | collective-permute-start | bytes 6152 | tf_op jit(solution)/shard_map/ppermute | solution.py:138
  9.3 4.6 %collective-permute-start.5 = (s32[2,2,128]{2,1,0:T(2,128)S(1)}, s32[2,2,128]{2,1,0:T(2,128)S(1)}, u32[]{:S(2)}, u32[]{:S(2)}) collective-permute-start(s32[2,2,128]{2,1,0:T(2,128)S(1)} %pad_add_fusion), channel_id=1, source_target_pairs={{0,4},{1,5},{2,6},{3,7},{4,0},{5,1},{6,2},{7,3},{8,12},{9,13},{10,... | collective-permute-start | bytes 6152 | tf_op jit(solution)/shard_map/ppermute | solution.py:138
  9.6 4.4 %collective-permute-start.7 = (bf16[2,2,16,640]{3,2,1,0:T(8,128)(2,1)S(1)}, bf16[2,2,16,640]{3,2,1,0:T(8,128)(2,1)S(1)}, u32[]{:S(2)}, u32[]{:S(2)}) collective-permute-start(bf16[2,2,16,640]{3,2,1,0:T(8,128)(2,1)S(1)} %get-tuple-element.6), channel_id=1, source_target_pairs={{0,1},{1,0},{2,3},{3,2},{4,5},{5,4},{6,7},{7,6},{8,9},{9,8},{10,11... | collective-permute-start | bytes 245768 | tf_op jit(solution)/shard_map/ppermute | solution.py:160
  10.8 5.7 %collective-permute-start.8 = (bf16[2,2,16,640]{3,2,1,0:T(8,128)(2,1)S(1)}, bf16[2,2,16,640]{3,2,1,0:T(8,128)(2,1)S(1)}, u32[]{:S(2)}, u32[]{:S(2)}) collective-permute-start(bf16[2,2,16,640]{3,2,1,0:T(8,128)(2,1)S(1)} %get-tuple-element.5), channel_id=1, source_target_pairs={{1,2},{2,1},{3,4},{4,3},{5,6},{6,5},{7,8},{8,7},{9,10},{10,9},{11,... | collective-permute-start | bytes 245768 | tf_op jit(solution)/shard_map/ppermute | solution.py:162
  14.0 2.5 %copy-start = (s32[2,2]{1,0:T(2,128)S(1)}, s32[2,2]{1,0:T(2,128)}, u32[]{:S(2)}) copy-start(s32[2,2]{1,0:T(2,128)} %refs_1_.1) | copy-start | bytes 52
